TPU v7x, 512 devices: a whole 4x8x8 slice. The times are simulated.
512 devices in a mesh: ctx: 4 (over z_hi), row: 8 (over x, core), col: 16 (over y, z_lo).
Axes of the slice: x: 4, y: 8, z: 8 (z_hi: 4, z_lo: 2; z = z_hi * 2 + z_lo), core: 2. Of those that a mesh axis runs over, the one named last changes fastest.
Arguments:
- tokens: bfloat16 [1024, 8192], P('ctx', 'row'), may hold values from -6 to 6
- proj_x: bfloat16 [8192, 8192], P('row', 'col'), may hold values from -0.09375 to 0.09375
- proj_z: bfloat16 [8192, 8192], P('row', 'col'), may hold values from -0.0625 to 0.0625
- proj_bc: bfloat16 [8192, 256], P('row'), may hold values from -0.015625 to 0.015625
- proj_dt: bfloat16 [8192, 128], P('row', 'col'), may hold values from -0.0625 to 0.0625
- dt_bias: float32 [128], P('col'), may hold values from -1.5 to 0.5
- decay_rate: float32 [128], P('col'), may hold values from 0.00048828125 to 0.2
- skip_gain: float32 [128], P('col'), may hold values from 0.5 to 1.5
- conv_x: float32 [8192, 4], P('col'), may hold values from -3 to 3
- conv_bc: float32 [256, 4], replicated, may hold values from -3 to 3
- norm_gain: float32 [8192], P('col'), may hold values from 0.1 to 1.9
- proj_out: bfloat16 [8192, 8192], P('col', 'row'), may hold values from -0.09375 to 0.09375
Outputs:
- layer_out: bfloat16 [1024, 8192], P('ctx', ('row', 'col'))
All inputs are finite; a program needn't handle non-finite values.
Results may differ from a plain program's by a relative error of at most 0.03.
Values may be sent and summed in bfloat16 or wider, within the bound.
A program may use at most 64 MiB of HBM per device.

v0:
```python
import jax
import jax.numpy as jnp
from jax import lax
from jax.sharding import PartitionSpec as P

Q = 256


highest_mode = lax.Precision.HIGHEST


def split_up(shard, dim, devices):
    before, after = (shard.shape[:dim], shard.shape[dim + 1 :])
    return jnp.moveaxis(shard.reshape(*before, devices, -1, *after), dim, 0)


def summed_on_arrival(shard, axis, dim):
    devices = lax.axis_size(axis)
    blocks = lax.all_to_all(split_up(shard, dim, devices), axis, 0, 0, tiled=True)
    return jnp.sum(blocks.astype(jnp.float32), axis=0)


def copy_for_each(shard, axis):
    copies = jnp.broadcast_to(shard, (lax.axis_size(axis), *shard.shape))
    return lax.all_to_all(copies, axis, split_axis=0, concat_axis=0, tiled=True)


def over_copies(shard, axis):
    return copy_for_each(shard, axis).astype(jnp.float32).sum(axis=0)


def shifted(shard, axis, by):
    devices = lax.axis_size(axis)
    pairs = [(i, i + by) for i in range(devices) if 0 <= i + by < devices]
    return lax.ppermute(shard, axis, pairs)


def all_in_one(shard, axis):
    leaves = jax.tree.leaves(shard)
    turns = sorted(range(len(leaves)), key=lambda k: -leaves[k].size)
    width = (1, *leaves[turns[0]].shape)[-1]
    lines = [
        jnp.pad(leaves[k].reshape(-1), (0, -leaves[k].size % width)).reshape(-1, width)
        for k in turns
    ]
    both, at, found = (copy_for_each(jnp.concatenate(lines), axis), 0, {})
    for k, line in zip(turns, lines):
        section = both[:, at : at + len(line)].reshape(len(both), -1)
        found[k] = section[:, : leaves[k].size].reshape(-1, *leaves[k].shape)
        at += len(line)
    numbers = iter(range(len(leaves)))
    return jax.tree.map(lambda _: found[next(numbers)], shard)


def joined_by_halves(pieces, combine):
    while len(jax.tree.leaves(pieces)[0]) > 1:
        pieces = jax.vmap(combine)(
            *(jax.tree.map(lambda part: part[side::2], pieces) for side in (0, 1))
        )
    return jax.tree.map(lambda part: part[0], pieces)


def entering(shard, axis, combine, identity):
    devices, place = (lax.axis_size(axis), lax.axis_index(axis))
    passed = jnp.arange(devices) < place

    def kept(part, zero, own):
        part = jnp.where(
            passed.reshape(-1, *(1 for _ in own.shape)),
            part.astype(own.dtype),
            jnp.asarray(zero, own.dtype),
        )
        return part

    pieces = all_in_one(
        jax.tree.map(lambda part, kind: part.astype(kind), shard, (jnp.bfloat16, jnp.bfloat16)),
        axis,
    )
    return joined_by_halves(jax.tree.map(kept, pieces, identity, shard), combine)


def laid_out(blocks, dim):
    blocks = jnp.moveaxis(blocks, 0, dim)
    lengths = blocks.shape
    return blocks.reshape(*lengths[:dim], lengths[dim] * lengths[dim + 1], *lengths[dim + 2 :])


def gathered_copies(shard, axis, dim):
    return laid_out(copy_for_each(shard, axis), dim)


def chain_combine(earlier, later):
    return (earlier[0] + later[0], jnp.exp(later[0])[:, None, None] * earlier[1] + later[1])


def local(
    tokens,
    proj_x,
    proj_z,
    proj_bc,
    proj_dt,
    dt_bias,
    decay_rate,
    skip_gain,
    conv_x,
    conv_bc,
    norm_gain,
    proj_out,
):
    tok_count = tokens.shape[0]
    col_heads = proj_dt.shape[1]
    head_dim = proj_x.shape[1] // col_heads
    state_dim = proj_bc.shape[1] // 2
    tap_count = conv_bc.shape[1]
    group_count = tok_count // Q
    bc_term = jnp.einsum("dc,td->ct", proj_bc, tokens, preferred_element_type=jnp.float32)
    local_heads = col_heads // lax.axis_size("row")
    first_head = lax.axis_index("row") * local_heads
    x_part = jnp.einsum("dc,td->ct", proj_x, tokens, preferred_element_type=jnp.float32).reshape(
        local_heads * lax.axis_size("row"), head_dim, tok_count
    )
    z_part = jnp.einsum("dc,td->ct", proj_z, tokens, preferred_element_type=jnp.float32).reshape(
        local_heads * lax.axis_size("row"), head_dim, tok_count
    )
    dt_part = jnp.einsum("dc,td->ct", proj_dt, tokens, preferred_element_type=jnp.float32).reshape(
        local_heads * lax.axis_size("row"), 1, tok_count
    )
    head_sum = summed_on_arrival(
        jnp.concatenate([x_part, z_part, dt_part], axis=1).astype(jnp.bfloat16), "row", 0
    )
    bc_sum = over_copies(bc_term.astype(jnp.bfloat16), "row").astype(jnp.float32)
    channels = local_heads * head_dim
    head_in = head_sum.astype(jnp.bfloat16)
    bc_in = bc_sum.astype(jnp.bfloat16)
    z_in = head_in[:, head_dim : 2 * head_dim]
    dt_in = head_in[:, 2 * head_dim]
    flat_in = jnp.concatenate([head_in[:, :head_dim].reshape(channels, tok_count), bc_in], axis=0)
    prior = shifted(flat_in[:, tok_count - tap_count + 1 :], "ctx", 1)
    padded = jnp.concatenate([prior, flat_in], axis=1).astype(jnp.float32)
    kernel = jnp.concatenate(
        [lax.dynamic_slice_in_dim(conv_x, first_head * head_dim, channels, 0), conv_bc], axis=0
    )
    running = jnp.zeros(flat_in.shape, jnp.float32)
    for tap_index in range(tap_count):
        running = (
            running
            + kernel[:, tap_index : tap_index + 1] * padded[:, tap_index : tap_index + tok_count]
        )
    conv_out = jax.nn.silu(running)
    x_conv = conv_out[:channels].reshape(local_heads, head_dim, tok_count)
    b_blocks = conv_out[channels : channels + state_dim].reshape(state_dim, group_count, Q)
    c_blocks = conv_out[channels + state_dim :].reshape(state_dim, group_count, Q)
    bias_now = lax.dynamic_slice_in_dim(dt_bias, first_head, local_heads, 0)
    decay_now = lax.dynamic_slice_in_dim(decay_rate, first_head, local_heads, 0)
    skip_now = lax.dynamic_slice_in_dim(skip_gain, first_head, local_heads, 0)
    gain_now = lax.dynamic_slice_in_dim(norm_gain, first_head * head_dim, channels, 0).reshape(
        local_heads, head_dim, 1
    )
    dt_full = jax.nn.softplus(dt_in.astype(jnp.float32) + bias_now[:, None])
    log_decay = -decay_now[:, None] * dt_full
    x_scaled = x_conv * dt_full[:, None, :]
    cum_decay = jnp.cumsum(log_decay.reshape(local_heads, group_count, Q), axis=2)
    x_blocks = x_scaled.reshape(local_heads, head_dim, group_count, Q)
    scores = jnp.einsum("nci,ncj->cij", c_blocks, b_blocks, precision=highest_mode)
    lower_mask = jnp.arange(Q)[:, None] >= jnp.arange(Q)[None, :]
    log_gap = cum_decay[:, :, :, None] - cum_decay[:, :, None, :]
    weights = jnp.where(lower_mask, jnp.exp(jnp.where(lower_mask, log_gap, 0.0)), 0.0)
    inner_out = jnp.einsum(
        "hcij,hpcj->hpci", scores[None] * weights, x_blocks, precision=highest_mode
    )
    tail_weight = jnp.exp(cum_decay[:, :, -1:] - cum_decay)
    group_states = jnp.einsum(
        "hcj,hpcj,ncj->chpn", tail_weight, x_blocks, b_blocks, precision=highest_mode
    )
    group_logs = cum_decay[:, :, -1].T

    def group_step(carried, step_inputs):
        group_log, group_state = step_inputs
        return (jnp.exp(group_log)[:, None, None] * carried + group_state, carried)

    start_state = jnp.zeros((local_heads, head_dim, state_dim), jnp.float32)
    final_state, local_enter = lax.scan(group_step, start_state, (group_logs, group_states))
    device_log = jnp.sum(group_logs, axis=0)
    before_logs = jnp.cumsum(group_logs, axis=0) - group_logs
    unused_log, device_state = entering(
        (device_log, final_state),
        "ctx",
        chain_combine,
        (jnp.zeros_like(device_log), jnp.zeros_like(final_state)),
    )
    enter_state = jnp.exp(before_logs)[:, :, None, None] * device_state[None] + local_enter
    outer_out = jnp.exp(cum_decay)[:, None] * jnp.einsum(
        "nci,chpn->hpci", c_blocks, enter_state, precision=highest_mode
    )
    ssm_out = (inner_out + outer_out).reshape(local_heads, head_dim, tok_count) + skip_now[
        :, None, None
    ] * x_conv
    gated = ssm_out * jax.nn.silu(z_in.astype(jnp.float32))
    inv_rms = lax.rsqrt(jnp.mean(gated * gated, axis=1, keepdims=True) + 1e-05)
    normed = (gated * inv_rms * gain_now).astype(jnp.bfloat16)
    out_cols = proj_out.shape[1]
    piece = gathered_copies(normed, "row", 0)
    piece_heads = piece.shape[0]
    rows_now = proj_out.reshape(piece_heads, head_dim, out_cols)
    col_partial = jnp.einsum("hpt,hpd->td", piece, rows_now, preferred_element_type=jnp.float32)
    return summed_on_arrival(col_partial.astype(jnp.bfloat16), "col", 1).astype(jnp.bfloat16)


def solution(mesh):
    in_specs = (
        P("ctx", "row"),
        P("row", "col"),
        P("row", "col"),
        P("row", None),
        P("row", "col"),
        P("col"),
        P("col"),
        P("col"),
        P("col", None),
        P(),
        P("col"),
        P("col", "row"),
    )
    out_specs = P("ctx", ("row", "col"))
    return jax.shard_map(local, mesh=mesh, in_specs=in_specs, out_specs=out_specs, check_vma=False)
```

profile of v0, /device:TPU:1, one launch (start us, length us, event | category | flops | bytes accessed | tf_op | source)
XLA Modules:
  0.0 108.6 jit_solution(3470042923757482811)
XLA Ops:
  0.0 1.4 %fusion.6 = bf16[8,1,1,256]{3,0,2,1:T(8,128)(2,1)S(1)} fusion(bf16[1024,8]{0,1:T(8,128)(2,1)} %param.16, bf16[256,1024]{1,0:T(8,128)(2,1)} %param.12), kind=kOutput, calls=%fused_computation.14 | convolution fusion | flops 4196352 | bytes 544768 | tf_op jit(solution)/shard_map/dc,td->ct/dot_general | solution.py:125
  1.4 2.0 %convolution_convert_fusion = bf16[512,256]{1,0:T(8,128)(2,1)S(1)} fusion(bf16[1024,512]{1,0:T(8,128)(2,1)} %param.14, bf16[256,1024]{1,0:T(8,128)(2,1)} %param.12), kind=kOutput, calls=%fused_computation.2 | convolution fusion | flops 268566528 | bytes 1835008 | tf_op jit(solution)/shard_map/dc,td->ct/dot_general | solution.py:122
  3.4 0.5 convolution_convert_fusion.1
  4.0 0.8 pad_maximum_fusion
  4.8 10.3 %all-to-all-start = ((bf16[8,1,129,256]{3,2,1,0:T(8,128)(2,1)}), bf16[8,1,129,256]{3,2,1,0:T(8,128)(2,1)S(1)}, u32[]{:S(2)}, u32[]{:S(2)}) async-start(bf16[8,1,129,256]{3,2,1,0:T(8,128)(2,1)} %pad_maximum_fusion), calls=%async_computation | async-start | bytes 1114112 | tf_op jit(solution)/shard_map/all_to_all | solution.py:19
  15.1 0.6 dynamic_slice.24
  15.7 0.7 dynamic_slice.22
  16.3 0.6 dynamic_slice.23
  17.5 0.8 dynamic_slice.25
  18.2 0.8 constant_dynamic-slice_fusion
  19.1 0.3 convolution_convert_fusion.2
  19.5 5.3 %all-to-all-done = bf16[8,1,129,256]{3,2,1,0:T(8,128)(2,1)S(1)} async-done(((bf16[8,1,129,256]{3,2,1,0:T(8,128)(2,1)}), bf16[8,1,129,256]{3,2,1,0:T(8,128)(2,1)S(1)}, u32[]{:S(2)}, u32[]{:S(2)}) %all-to-all-start) | async-done | bytes 528416 | tf_op jit(solution)/shard_map/all_to_all | solution.py:19
  24.8 1.1 broadcast_in_dim.35
  25.9 4.4 %all-to-all-start.1 = ((bf16[8,256,256]{2,1,0:T(8,128)(2,1)}), bf16[8,256,256]{2,1,0:T(8,128)(2,1)S(1)}, u32[]{:S(2)}, u32[]{:S(2)}) async-start(bf16[8,256,256]{2,1,0:T(8,128)(2,1)} %broadcast_in_dim.35), calls=%async_computation.1 | async-start | bytes 2097152 | tf_op jit(solution)/shard_map/all_to_all | solution.py:25
  30.4 0.7 compare_select_fusion
  31.8 0.6 slice.131
  32.4 0.7 slice.132
  34.4 10.8 %all-to-all-done.1 = bf16[8,256,256]{2,1,0:T(8,128)(2,1)S(1)} async-done(((bf16[8,256,256]{2,1,0:T(8,128)(2,1)}), bf16[8,256,256]{2,1,0:T(8,128)(2,1)S(1)}, u32[]{:S(2)}, u32[]{:S(2)}) %all-to-all-start.1) | async-done | bytes 1048608 | tf_op jit(solution)/shard_map/all_to_all | solution.py:25
  45.5 1.3 %collective-permute-start = (bf16[320,3]{1,0:T(8,128)(2,1)S(1)}, bf16[320,3]{1,0:T(8,128)(2,1)S(1)}, u32[]{:S(2)}, u32[]{:S(2)}) collective-permute-start(bf16[320,3]{1,0:T(8,128)(2,1)S(1)} %pad_maximum_fusion.1), channel_id=1, source_target_pairs={{0,128},{128,256},{256,384},{1,129},{129,257},{257,385},{2,130},{1... | collective-permute-start | bytes 5768 | tf_op jit(solution)/shard_map/ppermute | solution.py:35
  46.9 1.4 %collective-permute-done = bf16[320,3]{1,0:T(8,128)(2,1)S(1)} collective-permute-done((bf16[320,3]{1,0:T(8,128)(2,1)S(1)}, bf16[320,3]{1,0:T(8,128)(2,1)S(1)}, u32[]{:S(2)}, u32[]{:S(2)}) %collective-permute-start) | collective-permute-done | bytes 1952 | tf_op jit(solution)/shard_map/ppermute | solution.py:35
  48.4 0.5 divide_multiply_fusion
  49.0 0.4 convolution_multiply_fusion
  49.7 0.6 broadcast_in_dim.55
  50.3 10.6 %all-to-all-start.2 = ((bf16[4,65,128]{2,1,0:T(8,128)(2,1)}), bf16[4,65,128]{2,1,0:T(8,128)(2,1)S(1)}, u32[]{:S(2)}, u32[]{:S(2)}) async-start(bf16[4,65,128]{2,1,0:T(8,128)(2,1)} %broadcast_in_dim.55), calls=%async_computation.2 | async-start | bytes 147456 | tf_op jit(solution)/shard_map/all_to_all | solution.py:25
  60.9 0.4 fusion.19
  61.3 6.6 %all-to-all-done.2 = bf16[4,65,128]{2,1,0:T(8,128)(2,1)S(1)} async-done(((bf16[4,65,128]{2,1,0:T(8,128)(2,1)}), bf16[4,65,128]{2,1,0:T(8,128)(2,1)S(1)}, u32[]{:S(2)}, u32[]{:S(2)}) %all-to-all-start.2) | async-done | bytes 66592 | tf_op jit(solution)/shard_map/all_to_all | solution.py:25
  68.1 0.6 slice.109
  69.6 0.9 multiply_reduce_fusion
  70.5 12.1 %all_to_all.25 = bf16[8,1,64,256]{3,2,1,0:T(8,128)(2,1)S(1)} all-to-all(bf16[8,1,64,256]{3,2,1,0:T(8,128)(2,1)S(1)} %broadcast_in_dim.59), channel_id=1, replica_groups=mesh['ctx'=4,'row'=8,'col'=16] {'row'}, dimensions={0} | all-to-all | bytes 524288 | tf_op jit(solution)/shard_map/all_to_all | solution.py:25
  82.6 0.5 fusion
  83.3 24.6 %all_to_all.26 = bf16[16,256,64]{1,2,0:T(8,128)(2,1)S(1)} all-to-all(bf16[16,256,64]{1,2,0:T(8,128)(2,1)S(1)} %bitcast.79), channel_id=1, replica_groups=mesh['ctx'=4,'row'=8,'col'=16] {'col'}, dimensions={0} | all-to-all | bytes 1048576 | tf_op jit(solution)/shard_map/all_to_all | solution.py:19
  107.9 0.7 reduce_sum.55
  (47 shorter events, 2.4 us)
Async XLA Ops:
  0.0 82.6 %copy-start = (bf16[512,1024]{1,0:T(8,128)(2,1)S(1)}, bf16[512,1024]{1,0:T(8,128)(2,1)}, u32[]{:S(2)}) copy-start(bf16[512,1024]{1,0:T(8,128)(2,1)} %param.23) | copy-start | bytes 3145732
  1.4 2.0 %copy-start.1 = (bf16[256,1024]{1,0:T(8,128)(2,1)S(1)}, bf16[256,1024]{1,0:T(8,128)(2,1)}, u32[]{:S(2)}) copy-start(bf16[256,1024]{1,0:T(8,128)(2,1)} %param.12) | copy-start | bytes 1572868
  1.4 2.0 %copy-start.4 = (bf16[1024,512]{1,0:T(8,128)(2,1)S(1)}, bf16[1024,512]{1,0:T(8,128)(2,1)}, u32[]{:S(2)}) copy-start(bf16[1024,512]{1,0:T(8,128)(2,1)} %param.13) | copy-start | bytes 3145732
  3.9 11.2 %copy-start.5 = (f32[8]{0:T(128)S(1)}, f32[8]{0:T(128)}, u32[]{:S(2)}) copy-start(f32[8]{0:T(128)} %param.19) | copy-start | bytes 100
  3.9 11.7 %copy-start.6 = (f32[8]{0:T(128)S(1)}, f32[8]{0:T(128)}, u32[]{:S(2)}) copy-start(f32[8]{0:T(128)} %param.17) | copy-start | bytes 100
  3.9 12.4 %copy-start.7 = (f32[8]{0:T(128)S(1)}, f32[8]{0:T(128)}, u32[]{:S(2)}) copy-start(f32[8]{0:T(128)} %param.18) | copy-start | bytes 100
  3.9 15.0 %copy-start.3 = (f32[256,4]{0,1:T(4,128)S(1)}, f32[256,4]{0,1:T(4,128)}, u32[]{:S(2)}) copy-start(f32[256,4]{0,1:T(4,128)} %param.21) | copy-start | bytes 12292
  4.0 15.2 %copy-start.2 = (bf16[1024,256]{1,0:T(8,128)(2,1)S(1)}, bf16[1024,256]{1,0:T(8,128)(2,1)}, u32[]{:S(2)}) copy-start(bf16[1024,256]{1,0:T(8,128)(2,1)} %param.15) | copy-start | bytes 1572868
  4.8 20.0 %all-to-all-start = ((bf16[8,1,129,256]{3,2,1,0:T(8,128)(2,1)}), bf16[8,1,129,256]{3,2,1,0:T(8,128)(2,1)S(1)}, u32[]{:S(2)}, u32[]{:S(2)}) async-start(bf16[8,1,129,256]{3,2,1,0:T(8,128)(2,1)} %pad_maximum_fusion), calls=%async_computation | async-start | bytes 1114112 | tf_op jit(solution)/shard_map/all_to_all | solution.py:19
  25.9 19.4 %all-to-all-start.1 = ((bf16[8,256,256]{2,1,0:T(8,128)(2,1)}), bf16[8,256,256]{2,1,0:T(8,128)(2,1)S(1)}, u32[]{:S(2)}, u32[]{:S(2)}) async-start(bf16[8,256,256]{2,1,0:T(8,128)(2,1)} %broadcast_in_dim.35), calls=%async_computation.1 | async-start | bytes 2097152 | tf_op jit(solution)/shard_map/all_to_all | solution.py:25
  45.5 2.8 %collective-permute-start = (bf16[320,3]{1,0:T(8,128)(2,1)S(1)}, bf16[320,3]{1,0:T(8,128)(2,1)S(1)}, u32[]{:S(2)}, u32[]{:S(2)}) collective-permute-start(bf16[320,3]{1,0:T(8,128)(2,1)S(1)} %pad_maximum_fusion.1), channel_id=1, source_target_pairs={{0,128},{128,256},{256,384},{1,129},{129,257},{257,385},{2,130},{1... | collective-permute-start | bytes 5768 | tf_op jit(solution)/shard_map/ppermute | solution.py:35
  50.3 17.6 %all-to-all-start.2 = ((bf16[4,65,128]{2,1,0:T(8,128)(2,1)}), bf16[4,65,128]{2,1,0:T(8,128)(2,1)S(1)}, u32[]{:S(2)}, u32[]{:S(2)}) async-start(bf16[4,65,128]{2,1,0:T(8,128)(2,1)} %broadcast_in_dim.55), calls=%async_computation.2 | async-start | bytes 147456 | tf_op jit(solution)/shard_map/all_to_all | solution.py:25
where the time goes:
time: 109 us
  blocking collectives  36.7 us (34%)
  starting transfers between devices  26.6 us (24%)
  waiting for transfers between devices  24.1 us (22%)
  local copies, waits for them, and re-layouts  7.51 us (7%)
  matrix products  6.56 us (6%)
  other arithmetic  4.26 us (4%)
  between operations  2.87 us (3%)
    all_to_all x1, blocking collectives, summed_on_arrival(): lax.all_to_all(split_up(shard, dim, devices), axis, 0, 0, tiled=True)  24.6 us
    all_to_all x2, waiting for transfers between devices, copy_for_each(): return lax.all_to_all(copies, axis, split_axis=0, concat_axis=0, tiled=True)  17.4 us
    all_to_all x2, starting transfers between devices, copy_for_each(): return lax.all_to_all(copies, axis, split_axis=0, concat_axis=0, tiled=True)  15 us
    all_to_all x1, blocking collectives, copy_for_each(): return lax.all_to_all(copies, axis, split_axis=0, concat_axis=0, tiled=True)  12.1 us
    all_to_all x1, starting transfers between devices, summed_on_arrival(): lax.all_to_all(split_up(shard, dim, devices), axis, 0, 0, tiled=True)  10.3 us
    all_to_all x1, waiting for transfers between devices, summed_on_arrival(): lax.all_to_all(split_up(shard, dim, devices), axis, 0, 0, tiled=True)  5.33 us
  transfers between devices with their start and end apart: 4, of which 4 were waited for; matrix products, arithmetic and copies ran while one was open for 6% of the time, Pallas kernels for 0%

commit v1 on v0

v1 whole, which is shorter than its diff:
```python
import functools

import jax
import jax.numpy as jnp
from jax import lax
from jax.experimental import pallas as pl
from jax.experimental.pallas import tpu as pltpu
from jax.sharding import PartitionSpec as P

MESH = pl.DeviceIdType.MESH
F32 = jnp.float32
BF16 = jnp.bfloat16

N_CTX, N_ROW, N_COL = 4, 8, 16
N_X, N_Y = 4, 8
T = 256
KB = 1024
HD = 64
SLAB = 2 * HD + 16
TB = T // N_ROW
HAL = 8
FAR_FIRST_X = (2, 1, 3)
FAR_FIRST_Y = (4, 3, 5, 2, 6, 1, 7)


def dot(a, b):
    return jnp.dot(a, b, preferred_element_type=F32)


def dot_t(a, b):
    return lax.dot_general(a, b, (((1,), (1,)), ((), ())), preferred_element_type=F32)


def iota(shape, dim):
    return lax.broadcasted_iota(jnp.int32, shape, dim)


def silu(v):
    return v / (1.0 + jnp.exp(-v))


def kernel(
    tok_h, wx_h, wz_h, wbc_h, wdt_h, wout_h, cx_h, cbc_h, gain_h,
    bias_s, decay_s, skip_s,
    out_ref,
    tok, hal, wx, wz, wbc, wdt, wout, cx, cbc, gain,
    eye, tril, prm, prmt, wt,
    pbc, pxz, abc, axz, sbc, sxz, rbc, rxz, hs, hr, bcraw, bcf,
    st, sr, nb, os, ow, zr, ys, yr,
    sem_l, sem_hal,
    abc_s, abc_r, axz_s, axz_r, sbc_s, sbc_r, sxz_s, sxz_r, hr_s, hr_r,
    gbc_s, gbc_r, st_s, st_r, gn_s, gn_r, z_s, z_r, y_s, y_r,
):
    ctx = lax.axis_index("ctx")
    row = lax.axis_index("row")
    col = lax.axis_index("col")
    x, core = row // 2, row % 2
    y, zl = col // 2, col % 2

    def remote(src, dst, ss, rs, **peer):
        return pltpu.make_async_remote_copy(
            src_ref=src, dst_ref=dst, send_sem=ss, recv_sem=rs,
            device_id=peer, device_id_type=MESH,
        )

    barrier = pltpu.get_barrier_semaphore()

    def greet(**peer):
        pl.semaphore_signal(barrier, inc=1, device_id=peer, device_id_type=MESH)

    for d in range(1, N_CTX):
        greet(ctx=(ctx + d) % N_CTX)
    for d in FAR_FIRST_Y:
        greet(col=((y + d) % N_Y) * 2 + zl)
    for d in range(1, N_ROW):
        greet(row=(row + d) % N_ROW)
    greet(col=col + 1 - 2 * zl)

    loads = [
        pltpu.make_async_copy(src, dst, sem_l.at[k])
        for k, (src, dst) in enumerate(
            (
                (tok_h, tok), (wbc_h, wbc), (wx_h, wx), (wz_h, wz), (wdt_h, wdt),
                (wout_h, wout), (cx_h, cx), (cbc_h, cbc), (gain_h, gain),
            )
        )
    ]
    for load in loads:
        load.start()

    eye[...] = jnp.where(iota((T, T), 0) == iota((T, T), 1), 1.0, 0.0).astype(BF16)
    tril[...] = jnp.where(iota((T, T), 0) >= iota((T, T), 1), 1.0, 0.0).astype(BF16)
    prm[...] = jnp.zeros(prm.shape, F32)

    loads[0].wait()
    loads[1].wait()
    pbc[...] = dot(tok[...], wbc[...]).astype(BF16).reshape(N_ROW, TB, T)
    loads[4].wait()
    dt_part = dot_t(wdt[...], tok[...])
    for h in range(N_ROW):
        pxz[h, 2 * HD :, :] = jnp.broadcast_to(dt_part[h : h + 1], (16, T)).astype(BF16)
    for k, w in ((2, wx), (3, wz)):
        loads[k].wait()
        for b in range(2):
            part = dot(tok[...], w[:, b * T : (b + 1) * T]).astype(BF16)
            part = dot_t(eye[...], part).astype(BF16)
            for h in range(4):
                at = (k - 2) * HD
                pxz[4 * b + h, at : at + HD, :] = part[h * HD : (h + 1) * HD]

    pl.semaphore_wait(barrier, N_CTX - 1 + N_Y - 1 + N_ROW - 1 + 1)

    send_hal = remote(
        tok.at[pl.ds(T - HAL, HAL)], hal, sem_hal.at[0], sem_hal.at[1],
        ctx=(ctx + 1) % N_CTX,
    )

    @pl.when(ctx + 1 < N_CTX)
    def _():
        send_hal.start()

    def chip(d):
        return (x + d) % N_X

    order_a = FAR_FIRST_X + (0,)
    copies_abc = {
        d: remote(pbc.at[2 * chip(d) + 1 - core], abc.at[d], abc_s.at[d], abc_r.at[d], row=2 * x + 1 - core)
        for d in order_a
    }
    copies_axz = {
        d: remote(pxz.at[2 * chip(d) + 1 - core], axz.at[d], axz_s.at[d], axz_r.at[d], row=2 * x + 1 - core)
        for d in order_a
    }
    for d in order_a:
        copies_abc[d].start()
    for d in order_a:
        copies_axz[d].start()

    copies_sbc, copies_sxz = {}, {}
    for d in FAR_FIRST_X:
        copies_abc[d].wait_recv()
        sbc[d] = (pbc[2 * chip(d) + core].astype(F32) + abc[d].astype(F32)).astype(BF16)
        copies_sbc[d] = remote(sbc.at[d], rbc.at[d], sbc_s.at[d], sbc_r.at[d], row=2 * chip(d) + core)
        copies_sbc[d].start()
    for d in FAR_FIRST_X:
        copies_axz[d].wait_recv()
        sxz[d] = (pxz[2 * chip(d) + core].astype(F32) + axz[d].astype(F32)).astype(BF16)
        copies_sxz[d] = remote(sxz.at[d], rxz.at[d], sxz_s.at[d], sxz_r.at[d], row=2 * chip(d) + core)
        copies_sxz[d].start()

    @pl.when(ctx == 0)
    def _():
        hal[...] = jnp.zeros(hal.shape, BF16)

    @pl.when(ctx > 0)
    def _():
        send_hal.wait_recv()

    hal_bc = dot(hal[...], wbc[...]).astype(BF16)
    hal_x = dot(hal[...], wx[...]).astype(BF16)
    for b in range(2):
        hs[b, :HAL] = hal_bc
        hs[b, HAL:] = hal_x[:, b * T : (b + 1) * T]
    hr[row] = hs[row // 4]
    copies_hr = {}
    for d in range(1, N_ROW):
        to = (row + d) % N_ROW
        copies_hr[d] = remote(hs.at[to // 4], hr.at[row], hr_s.at[d], hr_r.at[d], row=to)
        copies_hr[d].start()

    copies_abc[0].wait_recv()
    bc_sum = pbc[row].astype(F32) + abc[0].astype(F32)
    for d in FAR_FIRST_X:
        copies_sbc[d].wait_recv()
        bc_sum += rbc[d].astype(F32)
    bcraw[row] = bc_sum.astype(BF16)
    copies_gbc = {}
    for d in range(1, N_ROW):
        copies_gbc[d] = remote(
            bcraw.at[row], bcraw.at[row], gbc_s.at[d], gbc_r.at[d], row=(row + d) % N_ROW
        )
        copies_gbc[d].start()

    for k in (6, 7, 8):
        loads[k].wait()
    lanes = pl.ds(pl.multiple_of((row // 2) * 128, 128), 128)
    prm[0:4, :] = cx[:, lanes]
    prm[4:5, :] = gain[:, lanes]
    prmt[...] = prm[...].T
    col_prm = prmt[pl.ds(pl.multiple_of((row % 2) * HD, HD), HD), :]

    loads[5].wait()
    for nb_ in range(4):
        for kb in range(2):
            block = dot_t(eye[...], wout[kb * T : (kb + 1) * T, nb_ * T : (nb_ + 1) * T]).astype(BF16)
            for s in range(4):
                wt[s % 2, 2 * nb_ + s // 2, :, kb * T : (kb + 1) * T] = block[s * HD : (s + 1) * HD]

    copies_axz[0].wait_recv()
    xz = pxz[row].astype(F32) + axz[0].astype(F32)
    for d in FAR_FIRST_X:
        copies_sxz[d].wait_recv()
        xz += rxz[d].astype(F32)
    x_in = xz[:HD]
    z_in = xz[HD : 2 * HD]
    dt_v = xz[2 * HD : 2 * HD + 8] + bias_s[row]
    dt8 = jnp.maximum(dt_v, 0.0) + jnp.log1p(jnp.exp(-jnp.abs(dt_v)))
    dt_row = dt8[0:1]

    log8 = dt8 * (-decay_s[row])
    hi = log8.astype(BF16).astype(F32)
    mid = (log8 - hi).astype(BF16).astype(F32)
    low = log8 - hi - mid
    sub = iota((8, T), 0)
    three = jnp.where(sub == 0, hi, jnp.where(sub == 1, mid, jnp.where(sub == 2, low, 0.0))).astype(BF16)
    cum_row = jnp.sum(dot_t(three, tril[...]), axis=0, keepdims=True)
    cum_col = jnp.sum(dot_t(tril[...], three), axis=1, keepdims=True)
    total = cum_row[:, T - 1 :]
    tail = jnp.exp(total - cum_row)
    gap = cum_col - cum_row
    keep = iota((T, T), 0) >= iota((T, T), 1)
    weights = jnp.where(keep, jnp.exp(jnp.where(keep, gap, 0.0)), 0.0)

    for d in range(1, N_ROW):
        copies_hr[d].wait_recv()
    halo = hr[0].astype(F32)
    for s in range(1, N_ROW):
        halo += hr[s].astype(F32)
    pick = jnp.where(iota((HD, T), 1) == (row % 4) * HD + iota((HD, T), 0), 1.0, 0.0).astype(BF16)
    before = jnp.concatenate([jnp.zeros((128 - HAL, T), F32), halo[HAL:]], axis=0).astype(BF16)
    x_before = dot_t(pick, before)

    x_cat = jnp.concatenate([x_before, x_in], axis=1)
    acc = col_prm[:, 3:4] * x_in
    for k in range(3):
        acc += col_prm[:, k : k + 1] * pltpu.roll(x_cat, 3 - k, 1)[:, 128:]
    x_conv = silu(acc)
    xs = x_conv * dt_row

    for d in range(1, N_ROW):
        copies_gbc[d].wait_recv()
    bcf[:HAL] = halo[:HAL]
    bcf[HAL:] = bcraw[...].reshape(T, T).astype(F32)
    acc = cbc[3:4, :] * bcf[HAL : HAL + T]
    for k in range(3):
        acc += cbc[k : k + 1, :] * bcf[HAL - 3 + k : HAL - 3 + k + T]
    bc_conv = silu(acc).astype(BF16)
    b_mat, c_mat = bc_conv[:, :128], bc_conv[:, 128:]

    state = dot((xs * tail).astype(BF16), b_mat)
    st[:HD] = state.astype(BF16)
    total_hi = total.astype(BF16).astype(F32)
    st[HD : HD + 8] = jnp.broadcast_to(total_hi, (8, 128)).astype(BF16)
    st[HD + 8 :] = jnp.broadcast_to(total - total_hi, (8, 128)).astype(BF16)
    copies_st = {
        d: remote(st, sr.at[d], st_s.at[d], st_r.at[d], ctx=(ctx + d) % N_CTX)
        for d in range(1, N_CTX)
    }
    for d in (2, 3, 1):
        @pl.when(ctx + d < N_CTX)
        def _():
            copies_st[d].start()

        @pl.when(ctx < d)
        def _():
            sr[d] = jnp.zeros(sr.shape[1:], BF16)

    scores = dot_t(c_mat, b_mat)
    inner = dot_t(xs.astype(BF16), (scores * weights).astype(BF16))
    partial_out = inner + skip_s[row] * x_conv
    gate = silu(z_in)
    for d in (1, 3, 2):
        @pl.when(ctx >= d)
        def _():
            copies_st[d].wait_recv()

    def log_of(d):
        return (sr[d, HD : HD + 8].astype(F32) + sr[d, HD + 8 :].astype(F32))[0:1]

    enter = sr[1, :HD].astype(F32)
    enter += jnp.exp(log_of(1)) * sr[2, :HD].astype(F32)
    enter += jnp.exp(log_of(1) + log_of(2)) * sr[3, :HD].astype(F32)
    outer = dot_t(enter.astype(BF16), c_mat) * jnp.exp(cum_row)
    gated = (partial_out + outer) * gate
    inv = lax.rsqrt(jnp.sum(gated * gated, axis=0, keepdims=True) * (1.0 / HD) + 1e-05)
    nb[row] = (gated * inv * col_prm[:, 4:5]).astype(BF16)

    copies_gn = {}
    for d in range(1, N_ROW):
        copies_gn[d] = remote(nb.at[row], nb.at[row], gn_s.at[d], gn_r.at[d], row=(row + d) % N_ROW)
        copies_gn[d].start()
    for d in range(1, N_ROW):
        copies_gn[d].wait_recv()

    heads = nb[...].reshape(N_ROW * HD, T)
    os[...] = dot(wt[1 - zl].reshape(N_Y * HD, N_ROW * HD), heads).astype(BF16).reshape(N_Y, HD, T)
    copies_z, copies_y = {}, {}
    for d in FAR_FIRST_Y + (0,):
        copies_z[d] = remote(
            os.at[(y + d) % N_Y], zr.at[d], z_s.at[d], z_r.at[d], col=col + 1 - 2 * zl
        )
        copies_z[d].start()
    ow[...] = dot(wt[zl].reshape(N_Y * HD, N_ROW * HD), heads).astype(BF16).reshape(N_Y, HD, T)
    for d in FAR_FIRST_Y:
        copies_z[d].wait_recv()
        ys[d] = (ow[(y + d) % N_Y].astype(F32) + zr[d].astype(F32)).astype(BF16)
        copies_y[d] = remote(ys.at[d], yr.at[d], y_s.at[d], y_r.at[d], col=((y + d) % N_Y) * 2 + zl)
        copies_y[d].start()
    copies_z[0].wait_recv()
    result = ow[y].astype(F32) + zr[0].astype(F32)
    for d in FAR_FIRST_Y:
        copies_y[d].wait_recv()
        result += yr[d].astype(F32)
    out_ref[...] = result.astype(BF16)

    @pl.when(ctx + 1 < N_CTX)
    def _():
        send_hal.wait_send()

    for d in range(1, N_CTX):
        @pl.when(ctx + d < N_CTX)
        def _():
            copies_st[d].wait_send()

    for group in (copies_abc, copies_axz, copies_sbc, copies_sxz, copies_hr, copies_gbc, copies_gn, copies_z, copies_y):
        for copy in group.values():
            copy.wait_send()


def scratch():
    vmem = pltpu.VMEM
    dma = lambda n: pltpu.SemaphoreType.DMA((n,))
    return [
        vmem((T, KB), BF16), vmem((HAL, KB), BF16), vmem((KB, 512), BF16), vmem((KB, 512), BF16),
        vmem((KB, 256), BF16), vmem((8, KB), BF16), vmem((512, KB), BF16),
        vmem((4, 512), F32), vmem((4, 256), F32), vmem((1, 512), F32),
        vmem((T, T), BF16), vmem((T, T), BF16), vmem((128, 128), F32), vmem((128, 128), F32),
        vmem((2, N_Y, HD, 512), BF16),
        vmem((N_ROW, TB, T), BF16), vmem((N_ROW, SLAB, T), BF16),
        vmem((N_X, TB, T), BF16), vmem((N_X, SLAB, T), BF16),
        vmem((N_X, TB, T), BF16), vmem((N_X, SLAB, T), BF16),
        vmem((N_X, TB, T), BF16), vmem((N_X, SLAB, T), BF16),
        vmem((2, 2 * HAL, T), BF16), vmem((N_ROW, 2 * HAL, T), BF16),
        vmem((N_ROW, TB, T), BF16), vmem((HAL + T, T), F32),
        vmem((HD + 16, 128), BF16), vmem((N_CTX, HD + 16, 128), BF16),
        vmem((N_ROW, HD, T), BF16), vmem((N_Y, HD, T), BF16), vmem((N_Y, HD, T), BF16),
        vmem((N_Y, HD, T), BF16), vmem((N_Y, HD, T), BF16), vmem((N_Y, HD, T), BF16),
        dma(9), dma(2),
        dma(4), dma(4), dma(4), dma(4), dma(4), dma(4), dma(4), dma(4), dma(8), dma(8),
        dma(8), dma(8), dma(4), dma(4), dma(8), dma(8), dma(8), dma(8), dma(8), dma(8),
    ]


def local(tokens, proj_x, proj_z, proj_bc, proj_dt, dt_bias, decay_rate, skip_gain, conv_x, conv_bc, norm_gain, proj_out):
    hbm = pl.BlockSpec(memory_space=pl.ANY)
    smem = pl.BlockSpec(memory_space=pltpu.SMEM)
    out = pl.pallas_call(
        kernel,
        out_shape=jax.ShapeDtypeStruct((HD, T), BF16),
        in_specs=[hbm] * 9 + [smem] * 3,
        out_specs=pl.BlockSpec(memory_space=pltpu.VMEM),
        scratch_shapes=scratch(),
        compiler_params=pltpu.CompilerParams(collective_id=0, has_side_effects=True),
    )(
        tokens, proj_x, proj_z, proj_bc, proj_dt.T, proj_out,
        conv_x.T, conv_bc.T, norm_gain.reshape(1, -1),
        dt_bias, decay_rate, skip_gain,
    )
    return out.T


def solution(mesh):
    in_specs = (
        P("ctx", "row"),
        P("row", "col"),
        P("row", "col"),
        P("row", None),
        P("row", "col"),
        P("col"),
        P("col"),
        P("col"),
        P("col", None),
        P(),
        P("col"),
        P("col", "row"),
    )
    out_specs = P("ctx", ("row", "col"))
    return jax.shard_map(local, mesh=mesh, in_specs=in_specs, out_specs=out_specs, check_vma=False)
```

time: 109 us -> 44.7 us (0.41)
  Pallas kernels: 0 us -> 43 us
  blocking collectives: 36.7 us -> 0 us
  starting transfers between devices: 26.6 us -> 0 us
  waiting for transfers between devices: 24.1 us -> 0 us
  matrix products: 6.56 us -> 0 us
  local copies, waits for them, and re-layouts: 7.51 us -> 1.38 us
  other arithmetic: 4.26 us -> 0 us
  between operations: 2.87 us -> 0.01 us
    pallas_call x0 -> x1, Pallas kernels: none -> 43 us  [local(): pl.pallas_call(kernel, out_shape=jax.ShapeDtypeStruct((HD, T), BF16), in_...]
    all_to_all x2 -> x0, blocking collectives: 36.7 us -> none  [the longest x1 24.6 us: summed_on_arrival(): lax.all_to_all(split_up(shard, dim, devices), axis, 0, 0, tiled=True)]
    all_to_all x3 -> x0, starting transfers between devices: 25.3 us -> none  [the longest x2 15 us: copy_for_each(): return lax.all_to_all(copies, axis, split_axis=0, concat_axis=0, tiled=True)]
    all_to_all x3 -> x0, waiting for transfers between devices: 22.7 us -> none  [the longest x2 17.4 us: copy_for_each(): return lax.all_to_all(copies, axis, split_axis=0, concat_axis=0, tiled=True)]
    dot_general x9 -> x0, matrix products: 6.56 us -> none  [the longest x1 1.96 us: local(): jnp.einsum('dc,td->ct', proj_z, tokens, preferred_element_type=jnp.float32)]
    dynamic_slice x5 -> x0, local copies, waits for them, and re-layouts: 3.34 us -> none  [the longest x1 0.76 us: local(): lax.dynamic_slice_in_dim(norm_gain, first_head * head_dim, channels, 0)]
    slice x7 -> x0, local copies, waits for them, and re-layouts: 2.09 us -> none  [the longest x2 1.25 us: local(): group_logs = cum_decay[:, :, -1].T]
    broadcast_in_dim x3 -> x0, local copies, waits for them, and re-layouts: 1.71 us -> none  [copy_for_each(): copies = jnp.broadcast_to(shard, (lax.axis_size(axis), *shard.shape))]
  transfers between devices with their start and end apart: 4 -> 0, of which waited for: 4 -> 0; matrix products, arithmetic and copies ran while one was open for 6% -> 0% of each run, Pallas kernels for 0% -> 0%
where the time goes in v1:
time: 44.7 us; the launch traced here: 44.4 us
  Pallas kernels  43 us (96%)
  local copies, waits for them, and re-layouts  1.38 us (3%)
    pallas_call x1, Pallas kernels, local(): pl.pallas_call(kernel, out_shape=jax.ShapeDtypeStruct((HD, T), BF16), in_...  43 us
    unnamed x1, local copies, waits for them, and re-layouts  1.38 us

profile of v1, /device:TPU:1, one launch (start us, length us, event | category | flops | bytes accessed | tf_op | source)
XLA Modules:
  0.0 44.4 jit_solution(10844973455090467021)
XLA Ops:
  0.0 43.0 %shard_map.118 = bf16[64,256]{1,0:T(8,128)(2,1)} custom-call(bf16[256,1024]{1,0:T(8,128)(2,1)} %tok_h.1, bf16[1024,512]{1,0:T(8,128)(2,1)} %wx_h.1, bf16[1024,512]{1,0:T(8,128)(2,1)} %wz_h.1, bf16[1024,256]{1,0:T(8,128)(2,1)} %wbc_h.1, bf16[8,1024]{1,0:T(8,128)(2,1)} %bitcast.6, bf16[512,1024]{1,0:T(8,128)(2,1)} %wout_h.1, f32[4,512]{1,0:T(4,128)} %bitcast.7, ...), custom_call_target="tpu_custom_call" | custom-call | tf_op jit(solution)/shard_map/pallas_call | solution.py:357
  43.0 1.4 %copy.14 = bf16[256,64]{0,1:T(8,128)(2,1)} copy(bf16[256,64]{0,1:T(8,128)(2,1)} %bitcast.5) | data formatting | bytes 65536

commit v2 on v1

v2 whole, which is shorter than its diff:
```python
import functools

import jax
import jax.numpy as jnp
from jax import lax
from jax.experimental import pallas as pl
from jax.experimental.pallas import tpu as pltpu
from jax.sharding import PartitionSpec as P

MESH = pl.DeviceIdType.MESH
F32 = jnp.float32
BF16 = jnp.bfloat16

N_CTX, N_ROW, N_COL = 4, 8, 16
N_X, N_Y = 4, 8
T = 256
KB = 1024
HD = 64
TB = T // N_ROW
HAL = 16
FAR_FIRST_Y = (4, 3, 5, 2, 6, 1, 7)


def dot(a, b):
    return jnp.dot(a, b, preferred_element_type=F32)


def dot_t(a, b):
    return lax.dot_general(a, b, (((1,), (1,)), ((), ())), preferred_element_type=F32)


def iota(shape, dim):
    return lax.broadcasted_iota(jnp.int32, shape, dim)


def silu(v):
    return v / (1.0 + jnp.exp(-v))


class Links:
    def __init__(self):
        self.started = []

    def when(self, cond, act):
        if cond is None:
            act()
        else:
            pl.when(cond)(act)

    def start(self, copy, cond_send=None, cond_recv=None):
        self.when(cond_send, copy.start)
        self.started.append([copy, cond_send, cond_recv, True])
        return len(self.started) - 1

    def arrive(self, k):
        copy, _, cond, waiting = self.started[k]
        if waiting:
            self.when(cond, copy.wait_recv)
            self.started[k][3] = False

    def finish(self):
        for k, (copy, cond, _, _) in enumerate(self.started):
            self.arrive(k)
            self.when(cond, copy.wait_send)


def kernel(
    tok_h, wx_h, wz_h, wbc_h, wdt_h, wout_h, cx_h, cbc_h, gain_h,
    bias_s, decay_s, skip_s,
    out_ref,
    tok, wx, wz, wbc, wdt, wout, cx, cbc, gain,
    eye, tril, prm, prmt, wt,
    pbc, px, pz, abc, ax, az, sbc, sx, sz, rbc, rx, rz, xt, xt_in, bt_in, bcraw, bcf,
    st, sr, nb, os, ow, zr, ys, yr,
    here_y, here_ctx, sem_l, tail_s, tail_r,
    abc_s, abc_r, ax_s, ax_r, az_s, az_r, sbc_s, sbc_r, sx_s, sx_r, sz_s, sz_r,
    gbc_s, gbc_r, st_s, st_r, gn_s, gn_r, z_s, z_r, y_s, y_r,
):
    ctx = lax.axis_index("ctx")
    row = lax.axis_index("row")
    col = lax.axis_index("col")
    x, core = row // 2, row % 2
    y, zl = col // 2, col % 2

    def remote(src, dst, ss, rs, **peer):
        return pltpu.make_async_remote_copy(
            src_ref=src, dst_ref=dst, send_sem=ss, recv_sem=rs,
            device_id=peer, device_id_type=MESH,
        )

    barrier = pltpu.get_barrier_semaphore()

    def greet(**peer):
        pl.semaphore_signal(barrier, inc=1, device_id=peer, device_id_type=MESH)

    def rank(at):
        return jnp.minimum(at, N_Y - at) * N_Y + at

    waits = N_ROW - 1 + 1 + ctx
    for d in range(1, N_ROW):
        greet(row=(row + d) % N_ROW)
    greet(col=col + 1 - 2 * zl)
    earlier = {}
    for d in range(1, N_Y):
        peer = (y + d) % N_Y
        earlier[d] = rank(peer) < rank(y)
        waits += earlier[d].astype(jnp.int32)
        pl.when(jnp.logical_not(earlier[d]))(lambda: greet(col=peer * 2 + zl))
    for d in range(1, N_CTX):
        pl.when(ctx + d < N_CTX)(lambda: greet(ctx=ctx + d))

    def enter():
        pl.semaphore_wait(barrier, waits)
        for d in range(1, N_Y):
            peer = ((y + d) % N_Y) * 2 + zl
            pl.when(earlier[d])(
                lambda: pl.semaphore_signal(here_y, inc=1, device_id={"col": peer}, device_id_type=MESH)
            )
        for d in range(1, N_CTX):
            pl.when(ctx >= d)(
                lambda: pl.semaphore_signal(here_ctx.at[d], inc=1, device_id={"ctx": ctx - d}, device_id_type=MESH)
            )

    def present_y():
        if not seen["y"]:
            seen["y"] = True
            later = N_Y - 1 - (waits - N_ROW - ctx)
            pl.when(later > 0)(lambda: pl.semaphore_wait(here_y, later))

    def present_ctx(d):
        if d not in seen:
            seen[d] = True
            pl.when(ctx + d < N_CTX)(lambda: pl.semaphore_wait(here_ctx.at[d], 1))

    seen = {"y": False}
    b0 = ((x + 2) % N_X) // 2
    cols_of = lambda b: pl.ds(pl.multiple_of(b * T, T), T)
    loads = [
        pltpu.make_async_copy(src, dst, sem_l.at[k])
        for k, (src, dst) in enumerate(
            (
                (tok_h, tok), (wbc_h, wbc), (wdt_h, wdt),
                (wx_h.at[:, cols_of(b0)], wx.at[0]), (wx_h.at[:, cols_of(1 - b0)], wx.at[1]),
                (wz_h.at[:, cols_of(b0)], wz.at[0]), (wz_h.at[:, cols_of(1 - b0)], wz.at[1]),
                (cx_h, cx), (cbc_h, cbc), (gain_h, gain), (wout_h, wout),
            )
        )
    ]
    links = Links()
    pending = set()

    def fetch(*ks):
        for k in ks:
            pending.add(k)
            loads[k].start()

    fetch(0, 1, 2, 3, 4)

    def need(*ks):
        for k in ks:
            if k in pending:
                pending.remove(k)
                loads[k].wait()

    def done():
        need(*tuple(pending))
        present_y()
        for d in range(1, N_CTX):
            present_ctx(d)
        links.finish()

    eye[...] = jnp.where(iota((T, T), 0) == iota((T, T), 1), 1.0, 0.0).astype(BF16)
    tril[...] = jnp.where(iota((T, T), 0) >= iota((T, T), 1), 1.0, 0.0).astype(BF16)
    prm[...] = jnp.zeros(prm.shape, F32)

    need(0, 1)
    pbc[...] = dot(tok[...], wbc[...]).astype(BF16).reshape(N_ROW, TB, T)
    fetch(5, 6, 7, 8, 9)
    need(2)
    dt_part = dot_t(wdt[...], tok[...])
    for h in range(N_ROW):
        px[h, HD:, :] = jnp.broadcast_to(dt_part[h : h + 1], (16, T)).astype(BF16)
    enter()

    odd = x % 2
    order = (2, 3 - 2 * odd, 1 + 2 * odd, 0)

    def chip(d):
        return (x + d) % N_X

    def to_sibling(part, into, ss, rs, d):
        return links.start(remote(part.at[2 * chip(d) + 1 - core], into.at[d], ss.at[d], rs.at[d], row=2 * x + 1 - core))

    def across(part, from_sibling, out, into, ss, rs, d):
        out[d] = (part[2 * chip(d) + core].astype(F32) + from_sibling[d].astype(F32)).astype(BF16)
        return links.start(remote(out.at[d], into.at[d], ss.at[d], rs.at[d], row=2 * chip(d) + core))

    def project(w, half, part):
        head = 4 * (b0 + half * (1 - 2 * b0))
        sums = dot(tok[...], w[half]).astype(BF16)
        sums = dot_t(eye[...], sums).astype(BF16)
        for h in range(4):
            part[head + h, :HD, :] = sums[h * HD : (h + 1) * HD]

    i_abc = [to_sibling(pbc, abc, abc_s, abc_r, d) for d in order]
    need(3)
    project(wx, 0, px)
    i_ax = [to_sibling(px, ax, ax_s, ax_r, d) for d in order[:2]]
    i_sbc = []
    for k, d in enumerate(order[:3]):
        links.arrive(i_abc[k])
        i_sbc.append(across(pbc, abc, sbc, rbc, sbc_s, sbc_r, d))
    need(4)
    project(wx, 1, px)
    i_ax += [to_sibling(px, ax, ax_s, ax_r, d) for d in order[2:]]
    fetch(10)
    need(5)
    project(wz, 0, pz)
    i_az = [to_sibling(pz, az, az_s, az_r, d) for d in order[:2]]
    i_sx = []
    for k, d in enumerate(order[:2]):
        links.arrive(i_ax[k])
        i_sx.append(across(px, ax, sx, rx, sx_s, sx_r, d))
    need(6)
    project(wz, 1, pz)
    i_az += [to_sibling(pz, az, az_s, az_r, d) for d in order[2:]]
    links.arrive(i_ax[2])
    i_sx.append(across(px, ax, sx, rx, sx_s, sx_r, order[2]))

    links.arrive(i_abc[3])
    bc_sum = pbc[row].astype(F32) + abc[0].astype(F32)
    for k in range(3):
        links.arrive(i_sbc[k])
    for d in range(1, N_X):
        bc_sum += rbc[d].astype(F32)
    bcraw[row] = bc_sum.astype(BF16)
    sibling = 2 * x + 1 - core

    def give(part, peer, source, ss, rs, k):
        return links.start(remote(part.at[source], part.at[source], ss.at[k], rs.at[k], row=peer))

    def gather_start(part, ss, rs):
        sent = {d: give(part, 2 * chip(d) + core, row, ss, rs, d) for d in (2, 1, 3)}
        sent[0] = give(part, sibling, row, ss, rs, 0)
        return sent

    def gather_pass_on(part, ss, rs, sent):
        for d in (1, 3, 2):
            links.arrive(sent[d])
            sent[4 + d] = give(part, sibling, 2 * chip(N_X - d) + core, ss, rs, 4 + d)

    def gather_end(sent):
        for k in (0, 5, 7, 6):
            links.arrive(sent[k])

    i_gbc = gather_start(bcraw, gbc_s, gbc_r)
    i_sz = []
    for k, d in enumerate(order[:3]):
        links.arrive(i_az[k])
        i_sz.append(across(pz, az, sz, rz, sz_s, sz_r, d))

    need(7, 8, 9)
    lanes = pl.ds(pl.multiple_of((row // 2) * 128, 128), 128)
    prm[0:4, :] = cx[:, lanes]
    prm[4:5, :] = gain[:, lanes]
    prmt[...] = prm[...].T
    col_prm = prmt[pl.ds(pl.multiple_of((row % 2) * HD, HD), HD), :]

    need(10)
    for nb_ in range(4):
        for kb in range(2):
            block = dot_t(eye[...], wout[kb * T : (kb + 1) * T, nb_ * T : (nb_ + 1) * T]).astype(BF16)
            for s in range(4):
                wt[s % 2, 2 * nb_ + s // 2, :, kb * T : (kb + 1) * T] = block[s * HD : (s + 1) * HD]

    links.arrive(i_ax[3])
    x_sum = px[row].astype(F32) + ax[0].astype(F32)
    for k in range(3):
        links.arrive(i_sx[k])
    for d in range(1, N_X):
        x_sum += rx[d].astype(F32)
    x_in = x_sum[:HD]
    xt[...] = x_in[:, 128:].astype(BF16)
    has_next, has_prior = ctx + 1 < N_CTX, ctx > 0
    present_ctx(1)
    i_xt = links.start(
        remote(xt, xt_in, tail_s.at[0], tail_r.at[0], ctx=(ctx + 1) % N_CTX), has_next, has_prior
    )

    @pl.when(ctx == 0)
    def _():
        xt_in[...] = jnp.zeros(xt_in.shape, BF16)
        bt_in[...] = jnp.zeros(bt_in.shape, BF16)

    dt_v = x_sum[HD : HD + 8] + bias_s[row]
    dt8 = jnp.maximum(dt_v, 0.0) + jnp.log1p(jnp.exp(-jnp.abs(dt_v)))
    dt_row = dt8[0:1]

    log8 = dt8 * (-decay_s[row])
    hi = log8.astype(BF16).astype(F32)
    mid = (log8 - hi).astype(BF16).astype(F32)
    low = log8 - hi - mid
    sub = iota((8, T), 0)
    three = jnp.where(sub == 0, hi, jnp.where(sub == 1, mid, jnp.where(sub == 2, low, 0.0))).astype(BF16)
    cum_row = jnp.sum(dot_t(three, tril[...]), axis=0, keepdims=True)
    cum_col = jnp.sum(dot_t(tril[...], three), axis=1, keepdims=True)
    total = cum_row[:, T - 1 :]
    tail = jnp.exp(total - cum_row)
    gap = cum_col - cum_row
    keep = iota((T, T), 0) >= iota((T, T), 1)
    weights = jnp.where(keep, jnp.exp(jnp.where(keep, gap, 0.0)), 0.0)

    gather_pass_on(bcraw, gbc_s, gbc_r, i_gbc)
    gather_end(i_gbc)
    i_bt = links.start(
        remote(bcraw.at[N_ROW - 1, pl.ds(TB - HAL, HAL)], bt_in, tail_s.at[1], tail_r.at[1], ctx=(ctx + 1) % N_CTX),
        has_next,
        has_prior,
    )

    links.arrive(i_xt)
    x_cat = jnp.concatenate([xt_in[...].astype(F32), x_in], axis=1)
    acc = col_prm[:, 3:4] * x_in
    for k in range(3):
        acc += col_prm[:, k : k + 1] * pltpu.roll(x_cat, 3 - k, 1)[:, 128:]
    x_conv = silu(acc)
    xs = x_conv * dt_row

    bcf[HAL:] = bcraw[...].reshape(T, T).astype(F32)
    links.arrive(i_bt)
    bcf[:HAL] = bt_in[...].astype(F32)
    acc = cbc[3:4, :] * bcf[HAL : HAL + T]
    for k in range(3):
        acc += cbc[k : k + 1, :] * bcf[HAL - 3 + k : HAL - 3 + k + T]
    bc_conv = silu(acc).astype(BF16)
    b_mat, c_mat = bc_conv[:, :128], bc_conv[:, 128:]

    state = dot((xs * tail).astype(BF16), b_mat)
    st[:HD] = state.astype(BF16)
    total_hi = total.astype(BF16).astype(F32)
    st[HD : HD + 8] = jnp.broadcast_to(total_hi, (8, 128)).astype(BF16)
    st[HD + 8 :] = jnp.broadcast_to(total - total_hi, (8, 128)).astype(BF16)
    i_st = {}
    for d in (2, 3, 1):
        present_ctx(d)
        copy = remote(st, sr.at[d], st_s.at[d], st_r.at[d], ctx=(ctx + d) % N_CTX)
        i_st[d] = links.start(copy, ctx + d < N_CTX, ctx >= d)

        @pl.when(ctx < d)
        def _():
            sr[d] = jnp.zeros(sr.shape[1:], BF16)

    scores = dot_t(c_mat, b_mat)
    inner = dot_t(xs.astype(BF16), (scores * weights).astype(BF16))
    partial_out = inner + skip_s[row] * x_conv
    links.arrive(i_az[3])
    z_in = pz[row].astype(F32) + az[0].astype(F32)
    for k in range(3):
        links.arrive(i_sz[k])
    for d in range(1, N_X):
        z_in += rz[d].astype(F32)
    gate = silu(z_in)
    for d in (1, 3, 2):
        links.arrive(i_st[d])

    def log_of(d):
        return (sr[d, HD : HD + 8].astype(F32) + sr[d, HD + 8 :].astype(F32))[0:1]

    enter = sr[1, :HD].astype(F32)
    enter += jnp.exp(log_of(1)) * sr[2, :HD].astype(F32)
    enter += jnp.exp(log_of(1) + log_of(2)) * sr[3, :HD].astype(F32)
    outer = dot_t(enter.astype(BF16), c_mat) * jnp.exp(cum_row)
    gated = (partial_out + outer) * gate
    inv = lax.rsqrt(jnp.sum(gated * gated, axis=0, keepdims=True) * (1.0 / HD) + 1e-05)
    nb[row] = (gated * inv * col_prm[:, 4:5]).astype(BF16)

    i_gn = gather_start(nb, gn_s, gn_r)
    gather_pass_on(nb, gn_s, gn_r, i_gn)
    gather_end(i_gn)

    heads = nb[...].reshape(N_ROW * HD, T)
    os[...] = dot(wt[1 - zl].reshape(N_Y * HD, N_ROW * HD), heads).astype(BF16).reshape(N_Y, HD, T)
    i_z, i_y = {}, {}
    for d in FAR_FIRST_Y + (0,):
        i_z[d] = links.start(remote(os.at[(y + d) % N_Y], zr.at[d], z_s.at[d], z_r.at[d], col=col + 1 - 2 * zl))
    ow[...] = dot(wt[zl].reshape(N_Y * HD, N_ROW * HD), heads).astype(BF16).reshape(N_Y, HD, T)
    present_y()
    for d in FAR_FIRST_Y:
        links.arrive(i_z[d])
        ys[d] = (ow[(y + d) % N_Y].astype(F32) + zr[d].astype(F32)).astype(BF16)
        i_y[d] = links.start(remote(ys.at[d], yr.at[d], y_s.at[d], y_r.at[d], col=((y + d) % N_Y) * 2 + zl))
    links.arrive(i_z[0])
    result = ow[y].astype(F32) + zr[0].astype(F32)
    for d in FAR_FIRST_Y:
        links.arrive(i_y[d])
        result += yr[d].astype(F32)
    out_ref[...] = result.astype(BF16)

    done()


def scratch():
    vmem = pltpu.VMEM
    dma = lambda n: pltpu.SemaphoreType.DMA((n,))
    return [
        vmem((T, KB), BF16), vmem((2, KB, T), BF16), vmem((2, KB, T), BF16),
        vmem((KB, 256), BF16), vmem((8, KB), BF16), vmem((512, KB), BF16),
        vmem((4, 512), F32), vmem((4, 256), F32), vmem((1, 512), F32),
        vmem((T, T), BF16), vmem((T, T), BF16), vmem((128, 128), F32), vmem((128, 128), F32),
        vmem((2, N_Y, HD, 512), BF16),
        *(vmem((n, rows, T), BF16) for n in (N_ROW, N_X, N_X, N_X) for rows in (TB, HD + 16, HD)),
        vmem((HD, 128), BF16), vmem((HD, 128), BF16), vmem((HAL, T), BF16),
        vmem((N_ROW, TB, T), BF16), vmem((HAL + T, T), F32),
        vmem((HD + 16, 128), BF16), vmem((N_CTX, HD + 16, 128), BF16),
        vmem((N_ROW, HD, T), BF16), vmem((N_Y, HD, T), BF16), vmem((N_Y, HD, T), BF16),
        vmem((N_Y, HD, T), BF16), vmem((N_Y, HD, T), BF16), vmem((N_Y, HD, T), BF16),
        pltpu.SemaphoreType.REGULAR, pltpu.SemaphoreType.REGULAR((N_CTX,)), dma(11), dma(2), dma(2),
        *(dma(4) for _ in range(12)),
        dma(8), dma(8), dma(4), dma(4), dma(8), dma(8), dma(8), dma(8), dma(8), dma(8),
    ]


def local(tokens, proj_x, proj_z, proj_bc, proj_dt, dt_bias, decay_rate, skip_gain, conv_x, conv_bc, norm_gain, proj_out):
    hbm = pl.BlockSpec(memory_space=pl.ANY)
    smem = pl.BlockSpec(memory_space=pltpu.SMEM)
    out = pl.pallas_call(
        kernel,
        out_shape=jax.ShapeDtypeStruct((HD, T), BF16),
        in_specs=[hbm] * 9 + [smem] * 3,
        out_specs=pl.BlockSpec(memory_space=pltpu.VMEM),
        scratch_shapes=scratch(),
        compiler_params=pltpu.CompilerParams(collective_id=0, has_side_effects=True),
    )(
        tokens, proj_x, proj_z, proj_bc, proj_dt.T, proj_out,
        conv_x.T, conv_bc.T, norm_gain.reshape(1, -1),
        dt_bias, decay_rate, skip_gain,
    )
    return out.T


def solution(mesh):
    in_specs = (
        P("ctx", "row"),
        P("row", "col"),
        P("row", "col"),
        P("row", None),
        P("row", "col"),
        P("col"),
        P("col"),
        P("col"),
        P("col", None),
        P(),
        P("col"),
        P("col", "row"),
    )
    out_specs = P("ctx", ("row", "col"))
    return jax.shard_map(local, mesh=mesh, in_specs=in_specs, out_specs=out_specs, check_vma=False)
```

time: 44.7 us -> 40.2 us (0.90)
  the two profiles are of different devices: /device:TPU:1 before, /device:TPU:384 now
where the time goes in v2:
time: 40.2 us; the launch traced here: 39.9 us
  Pallas kernels  38.6 us (96%)
  local copies, waits for them, and re-layouts  1.38 us (3%)
    pallas_call x1, Pallas kernels, local(): pl.pallas_call(kernel, out_shape=jax.ShapeDtypeStruct((HD, T), BF16), in_...  38.6 us
    unnamed x1, local copies, waits for them, and re-layouts  1.38 us

profile of v2, /device:TPU:384, one launch (start us, length us, event | category | flops | bytes accessed | tf_op | source)
XLA Modules:
  0.0 39.9 jit_solution(8294718739200646028)
XLA Ops:
  0.0 38.6 %shard_map.118 = bf16[64,256]{1,0:T(8,128)(2,1)} custom-call(bf16[256,1024]{1,0:T(8,128)(2,1)} %tok_h.1, bf16[1024,512]{1,0:T(8,128)(2,1)} %wx_h.1, bf16[1024,512]{1,0:T(8,128)(2,1)} %wz_h.1, bf16[1024,256]{1,0:T(8,128)(2,1)} %wbc_h.1, bf16[8,1024]{1,0:T(8,128)(2,1)} %bitcast.6, bf16[512,1024]{1,0:T(8,128)(2,1)} %wout_h.1, f32[4,512]{1,0:T(4,128)} %bitcast.7, ...), custom_call_target="tpu_custom_call" | custom-call | tf_op jit(solution)/shard_map/pallas_call | solution.py:426
  38.6 1.4 %copy.14 = bf16[256,64]{0,1:T(8,128)(2,1)} copy(bf16[256,64]{0,1:T(8,128)(2,1)} %bitcast.5) | data formatting | bytes 65536

commit v3 on v2

--- a/solution.py
+++ b/solution.py
@@ -18,7 +18,9 @@
 HD = 64
 TB = T // N_ROW
 HAL = 16
-FAR_FIRST_Y = (4, 3, 5, 2, 6, 1, 7)
+FAR_FIRST_ROW = (4, 3, 5, 2, 6, 1, 7)
+FOR_PARTNER = (4, 3, 5, 2, 6, 1, 7, 0)
+FOR_OWN = (1, 7, 4, 3, 5, 2, 6, 0)
 
 
 def dot(a, b):
@@ -31,6 +33,10 @@
 
 def iota(shape, dim):
     return lax.broadcasted_iota(jnp.int32, shape, dim)
+
+
+def rem(a, n):
+    return lax.rem(a, jnp.int32(n))
 
 
 def silu(v):
@@ -54,7 +60,7 @@
 
     def arrive(self, k):
         copy, _, cond, waiting = self.started[k]
-        if waiting:
+        if waiting and cond is not False:
             self.when(cond, copy.wait_recv)
             self.started[k][3] = False
 
@@ -66,21 +72,21 @@
 
 def kernel(
     tok_h, wx_h, wz_h, wbc_h, wdt_h, wout_h, cx_h, cbc_h, gain_h,
-    bias_s, decay_s, skip_s,
+    bias_h, decay_h, skip_h,
     out_ref,
     tok, wx, wz, wbc, wdt, wout, cx, cbc, gain,
-    eye, tril, prm, prmt, wt,
-    pbc, px, pz, abc, ax, az, sbc, sx, sz, rbc, rx, rz, xt, xt_in, bt_in, bcraw, bcf,
-    st, sr, nb, os, ow, zr, ys, yr,
-    here_y, here_ctx, sem_l, tail_s, tail_r,
-    abc_s, abc_r, ax_s, ax_r, az_s, az_r, sbc_s, sbc_r, sx_s, sx_r, sz_s, sz_r,
-    gbc_s, gbc_r, st_s, st_r, gn_s, gn_r, z_s, z_r, y_s, y_r,
+    bias_s, decay_s, skip_s, eye, tril, prm, prmt, wt,
+    pbc, px, pz, rbc, ax, az, sx, sz, rx, rz, xt, xt_in, bt_in, bcraw, bcf,
+    st, sr, nb, os, ow, zr, zs, yo, yh, yv, ys, yr,
+    here_y, here_ctx, sem_l, tail_s, tail_r, bt_s, bt_r,
+    bc_s, bc_r, ax_s, ax_r, az_s, az_r, sx_s, sx_r, sz_s, sz_r,
+    gbc_s, gbc_r, st_s, st_r, gn_s, gn_r, z_s, z_r, yo_s, yo_r, yh_s, yh_r, yv_s, yv_r, y_s, y_r,
 ):
     ctx = lax.axis_index("ctx")
     row = lax.axis_index("row")
     col = lax.axis_index("col")
-    x, core = row // 2, row % 2
-    y, zl = col // 2, col % 2
+    x, core = lax.div(row, 2), rem(row, 2)
+    y, zl = lax.div(col, 2), rem(col, 2)
 
     def remote(src, dst, ss, rs, **peer):
         return pltpu.make_async_remote_copy(
@@ -98,11 +104,11 @@
 
     waits = N_ROW - 1 + 1 + ctx
     for d in range(1, N_ROW):
-        greet(row=(row + d) % N_ROW)
+        greet(row=rem(row + d, N_ROW))
     greet(col=col + 1 - 2 * zl)
     earlier = {}
     for d in range(1, N_Y):
-        peer = (y + d) % N_Y
+        peer = rem(y + d, N_Y)
         earlier[d] = rank(peer) < rank(y)
         waits += earlier[d].astype(jnp.int32)
         pl.when(jnp.logical_not(earlier[d]))(lambda: greet(col=peer * 2 + zl))
@@ -112,7 +118,7 @@
     def enter():
         pl.semaphore_wait(barrier, waits)
         for d in range(1, N_Y):
-            peer = ((y + d) % N_Y) * 2 + zl
+            peer = (rem(y + d, N_Y)) * 2 + zl
             pl.when(earlier[d])(
                 lambda: pl.semaphore_signal(here_y, inc=1, device_id={"col": peer}, device_id_type=MESH)
             )
@@ -127,13 +133,11 @@
             later = N_Y - 1 - (waits - N_ROW - ctx)
             pl.when(later > 0)(lambda: pl.semaphore_wait(here_y, later))
 
-    def present_ctx(d):
-        if d not in seen:
-            seen[d] = True
-            pl.when(ctx + d < N_CTX)(lambda: pl.semaphore_wait(here_ctx.at[d], 1))
+    def present_ctx(d, cond):
+        pl.when(cond)(lambda: pl.semaphore_wait(here_ctx.at[d], 1))
 
     seen = {"y": False}
-    b0 = ((x + 2) % N_X) // 2
+    b0 = (rem(x + 2, N_X)) // 2
     cols_of = lambda b: pl.ds(pl.multiple_of(b * T, T), T)
     loads = [
         pltpu.make_async_copy(src, dst, sem_l.at[k])
@@ -143,6 +147,7 @@
                 (wx_h.at[:, cols_of(b0)], wx.at[0]), (wx_h.at[:, cols_of(1 - b0)], wx.at[1]),
                 (wz_h.at[:, cols_of(b0)], wz.at[0]), (wz_h.at[:, cols_of(1 - b0)], wz.at[1]),
                 (cx_h, cx), (cbc_h, cbc), (gain_h, gain), (wout_h, wout),
+                (bias_h, bias_s), (decay_h, decay_s), (skip_h, skip_s),
             )
         )
     ]
@@ -165,8 +170,6 @@
     def done():
         need(*tuple(pending))
         present_y()
-        for d in range(1, N_CTX):
-            present_ctx(d)
         links.finish()
 
     eye[...] = jnp.where(iota((T, T), 0) == iota((T, T), 1), 1.0, 0.0).astype(BF16)
@@ -175,18 +178,22 @@
 
     need(0, 1)
     pbc[...] = dot(tok[...], wbc[...]).astype(BF16).reshape(N_ROW, TB, T)
-    fetch(5, 6, 7, 8, 9)
+    fetch(5, 6, 7, 8, 9, 11, 12, 13)
+    enter()
+    i_bc = {}
+    for d in FAR_FIRST_ROW:
+        to = rem(row + d, N_ROW)
+        i_bc[d] = links.start(remote(pbc.at[to], rbc.at[d], bc_s.at[d], bc_r.at[d], row=to))
     need(2)
     dt_part = dot_t(wdt[...], tok[...])
     for h in range(N_ROW):
         px[h, HD:, :] = jnp.broadcast_to(dt_part[h : h + 1], (16, T)).astype(BF16)
-    enter()
 
     odd = x % 2
     order = (2, 3 - 2 * odd, 1 + 2 * odd, 0)
 
     def chip(d):
-        return (x + d) % N_X
+        return rem(x + d, N_X)
 
     def to_sibling(part, into, ss, rs, d):
         return links.start(remote(part.at[2 * chip(d) + 1 - core], into.at[d], ss.at[d], rs.at[d], row=2 * x + 1 - core))
@@ -202,14 +209,9 @@
         for h in range(4):
             part[head + h, :HD, :] = sums[h * HD : (h + 1) * HD]
 
-    i_abc = [to_sibling(pbc, abc, abc_s, abc_r, d) for d in order]
     need(3)
     project(wx, 0, px)
     i_ax = [to_sibling(px, ax, ax_s, ax_r, d) for d in order[:2]]
-    i_sbc = []
-    for k, d in enumerate(order[:3]):
-        links.arrive(i_abc[k])
-        i_sbc.append(across(pbc, abc, sbc, rbc, sbc_s, sbc_r, d))
     need(4)
     project(wx, 1, px)
     i_ax += [to_sibling(px, ax, ax_s, ax_r, d) for d in order[2:]]
@@ -227,11 +229,9 @@
     links.arrive(i_ax[2])
     i_sx.append(across(px, ax, sx, rx, sx_s, sx_r, order[2]))
 
-    links.arrive(i_abc[3])
-    bc_sum = pbc[row].astype(F32) + abc[0].astype(F32)
-    for k in range(3):
-        links.arrive(i_sbc[k])
-    for d in range(1, N_X):
+    bc_sum = pbc[row].astype(F32)
+    for d in FAR_FIRST_ROW:
+        links.arrive(i_bc[d])
         bc_sum += rbc[d].astype(F32)
     bcraw[row] = bc_sum.astype(BF16)
     sibling = 2 * x + 1 - core
@@ -253,13 +253,21 @@
         for k in (0, 5, 7, 6):
             links.arrive(sent[k])
 
-    i_gbc = gather_start(bcraw, gbc_s, gbc_r)
+    i_gbc = [give(bcraw, rem(row + d, N_ROW), row, gbc_s, gbc_r, d) for d in FAR_FIRST_ROW]
     i_sz = []
     for k, d in enumerate(order[:3]):
         links.arrive(i_az[k])
         i_sz.append(across(pz, az, sz, rz, sz_s, sz_r, d))
-
-    need(7, 8, 9)
+    has_next, has_prior, last_row = ctx + 1 < N_CTX, ctx > 0, row == N_ROW - 1
+    present_ctx(1, has_next & last_row)
+    i_bt = []
+    for to in range(N_ROW):
+        copy = remote(
+            bcraw.at[row, pl.ds(TB - HAL, HAL)], bt_in, bt_s.at[to], bt_r, ctx=rem(ctx + 1, N_CTX), row=to
+        )
+        i_bt.append(links.start(copy, has_next & last_row, has_prior if to == 0 else False))
+
+    need(7, 8, 9, 11, 12, 13)
     lanes = pl.ds(pl.multiple_of((row // 2) * 128, 128), 128)
     prm[0:4, :] = cx[:, lanes]
     prm[4:5, :] = gain[:, lanes]
@@ -267,11 +275,12 @@
     col_prm = prmt[pl.ds(pl.multiple_of((row % 2) * HD, HD), HD), :]
 
     need(10)
-    for nb_ in range(4):
-        for kb in range(2):
-            block = dot_t(eye[...], wout[kb * T : (kb + 1) * T, nb_ * T : (nb_ + 1) * T]).astype(BF16)
-            for s in range(4):
-                wt[s % 2, 2 * nb_ + s // 2, :, kb * T : (kb + 1) * T] = block[s * HD : (s + 1) * HD]
+    for d in range(N_Y):
+        lanes = pl.ds(pl.multiple_of((rem(y + d, N_Y)) * 128, 128), 128)
+        block = dot_t(eye[:128, :128], wout[:, lanes]).astype(BF16)
+        for side in range(2):
+            place = jnp.where(zl == side, N_Y + FOR_OWN.index(d), FOR_PARTNER.index(d))
+            wt[place] = block[side * HD : (side + 1) * HD]
 
     links.arrive(i_ax[3])
     x_sum = px[row].astype(F32) + ax[0].astype(F32)
@@ -281,10 +290,9 @@
         x_sum += rx[d].astype(F32)
     x_in = x_sum[:HD]
     xt[...] = x_in[:, 128:].astype(BF16)
-    has_next, has_prior = ctx + 1 < N_CTX, ctx > 0
-    present_ctx(1)
+    present_ctx(1, has_next & jnp.logical_not(last_row))
     i_xt = links.start(
-        remote(xt, xt_in, tail_s.at[0], tail_r.at[0], ctx=(ctx + 1) % N_CTX), has_next, has_prior
+        remote(xt, xt_in, tail_s.at[0], tail_r.at[0], ctx=rem(ctx + 1, N_CTX)), has_next, has_prior
     )
 
     @pl.when(ctx == 0)
@@ -310,13 +318,8 @@
     keep = iota((T, T), 0) >= iota((T, T), 1)
     weights = jnp.where(keep, jnp.exp(jnp.where(keep, gap, 0.0)), 0.0)
 
-    gather_pass_on(bcraw, gbc_s, gbc_r, i_gbc)
-    gather_end(i_gbc)
-    i_bt = links.start(
-        remote(bcraw.at[N_ROW - 1, pl.ds(TB - HAL, HAL)], bt_in, tail_s.at[1], tail_r.at[1], ctx=(ctx + 1) % N_CTX),
-        has_next,
-        has_prior,
-    )
+    for k in i_gbc:
+        links.arrive(k)
 
     links.arrive(i_xt)
     x_cat = jnp.concatenate([xt_in[...].astype(F32), x_in], axis=1)
@@ -327,7 +330,7 @@
     xs = x_conv * dt_row
 
     bcf[HAL:] = bcraw[...].reshape(T, T).astype(F32)
-    links.arrive(i_bt)
+    links.arrive(i_bt[0])
     bcf[:HAL] = bt_in[...].astype(F32)
     acc = cbc[3:4, :] * bcf[HAL : HAL + T]
     for k in range(3):
@@ -342,8 +345,9 @@
     st[HD + 8 :] = jnp.broadcast_to(total - total_hi, (8, 128)).astype(BF16)
     i_st = {}
     for d in (2, 3, 1):
-        present_ctx(d)
-        copy = remote(st, sr.at[d], st_s.at[d], st_r.at[d], ctx=(ctx + d) % N_CTX)
+        if d > 1:
+            present_ctx(d, ctx + d < N_CTX)
+        copy = remote(st, sr.at[d], st_s.at[d], st_r.at[d], ctx=rem(ctx + d, N_CTX))
         i_st[d] = links.start(copy, ctx + d < N_CTX, ctx >= d)
 
         @pl.when(ctx < d)
@@ -379,20 +383,63 @@
     gather_end(i_gn)
 
     heads = nb[...].reshape(N_ROW * HD, T)
-    os[...] = dot(wt[1 - zl].reshape(N_Y * HD, N_ROW * HD), heads).astype(BF16).reshape(N_Y, HD, T)
-    i_z, i_y = {}, {}
-    for d in FAR_FIRST_Y + (0,):
-        i_z[d] = links.start(remote(os.at[(y + d) % N_Y], zr.at[d], z_s.at[d], z_r.at[d], col=col + 1 - 2 * zl))
-    ow[...] = dot(wt[zl].reshape(N_Y * HD, N_ROW * HD), heads).astype(BF16).reshape(N_Y, HD, T)
+
+    def blocks(first, into, at):
+        part = dot(wt[first : first + 4].reshape(4 * HD, N_ROW * HD), heads)
+        into[at : at + 4] = part.astype(BF16).reshape(4, HD, T)
+
+    def to_partner(src, k):
+        return links.start(remote(src, zr.at[k], z_s.at[k], z_r.at[k], col=col + 1 - 2 * zl))
+
+    def along_y_to(src, into, ss, rs, d):
+        return links.start(remote(src, into, ss, rs, col=(rem(y + d, N_Y)) * 2 + zl))
+
+    def along_y(src, into, ss, rs, d):
+        return along_y_to(src, into.at[d], ss.at[d], rs.at[d], d)
+
+    blocks(0, os, 0)
+    i_z = [to_partner(os.at[k], k) for k in range(4)]
+    blocks(4, os, 4)
+    i_z.append(to_partner(os.at[4], 4))
     present_y()
-    for d in FAR_FIRST_Y:
-        links.arrive(i_z[d])
-        ys[d] = (ow[(y + d) % N_Y].astype(F32) + zr[d].astype(F32)).astype(BF16)
-        i_y[d] = links.start(remote(ys.at[d], yr.at[d], y_s.at[d], y_r.at[d], col=((y + d) % N_Y) * 2 + zl))
-    links.arrive(i_z[0])
-    result = ow[y].astype(F32) + zr[0].astype(F32)
-    for d in FAR_FIRST_Y:
-        links.arrive(i_y[d])
+    i_yo = [along_y(os.at[FOR_PARTNER.index(d)], yo, yo_s, yo_r, d) for d in (1, 7)]
+    blocks(N_Y, ow, 0)
+    i_y = [along_y(ow.at[FOR_OWN.index(d)], yr, y_s, y_r, d) for d in (1, 7)]
+    blocks(N_Y + 4, ow, 4)
+    i_near = {}
+    for k, d in enumerate(FOR_PARTNER[:5]):
+        if k == 2:
+            links.arrive(i_yo[0])
+            links.arrive(i_yo[1])
+            zs[...] = (os[7].astype(F32) + yo[1].astype(F32) + yo[7].astype(F32)).astype(BF16)
+            i_z0 = to_partner(zs, 7)
+        links.arrive(i_z[k])
+        own = ow[FOR_OWN.index(d)].astype(F32) + zr[k].astype(F32)
+        if d not in (2, 6):
+            ys[d] = own.astype(BF16)
+        if d in (3, 5):
+            to, on = (1, 2) if d == 3 else (7, 6)
+            i_near[on] = along_y_to(ys.at[d], yv.at[on], yv_s.at[on], yv_r.at[on], to)
+            continue
+        if d == 4:
+            i_half = {}
+            for to, at in ((2, 0), (6, HD // 2)):
+                rows = pl.ds(at, HD // 2)
+                i_half[to] = along_y_to(ys.at[4, rows], yh.at[rows], yh_s.at[to], yh_r.at[to], to)
+            continue
+        if d in (2, 6):
+            links.arrive(i_half[d])
+            links.arrive(i_near[d])
+            lo = slice(0, HD // 2), slice(HD // 2, HD)
+            for side, rows in ((2, lo[0]), (6, lo[1])):
+                more = own[rows] + yv[d, rows].astype(F32)
+                ys[d, rows] = (more + yh[rows].astype(F32) if side == d else more).astype(BF16)
+        i_y.append(along_y(ys.at[d], yr, y_s, y_r, d))
+    links.arrive(i_z0)
+    result = ow[7].astype(F32) + zr[7].astype(F32)
+    for k in i_y:
+        links.arrive(k)
+    for d in (1, 2, 6, 7):
         result += yr[d].astype(F32)
     out_ref[...] = result.astype(BF16)
 
@@ -406,28 +453,30 @@
         vmem((T, KB), BF16), vmem((2, KB, T), BF16), vmem((2, KB, T), BF16),
         vmem((KB, 256), BF16), vmem((8, KB), BF16), vmem((512, KB), BF16),
         vmem((4, 512), F32), vmem((4, 256), F32), vmem((1, 512), F32),
+        pltpu.SMEM((8,), F32), pltpu.SMEM((8,), F32), pltpu.SMEM((8,), F32),
         vmem((T, T), BF16), vmem((T, T), BF16), vmem((128, 128), F32), vmem((128, 128), F32),
-        vmem((2, N_Y, HD, 512), BF16),
-        *(vmem((n, rows, T), BF16) for n in (N_ROW, N_X, N_X, N_X) for rows in (TB, HD + 16, HD)),
+        vmem((2 * N_Y, HD, 512), BF16),
+        vmem((N_ROW, TB, T), BF16), vmem((N_ROW, HD + 16, T), BF16), vmem((N_ROW, HD, T), BF16),
+        vmem((N_ROW, TB, T), BF16),
+        *(vmem((N_X, rows, T), BF16) for _ in range(3) for rows in (HD + 16, HD)),
         vmem((HD, 128), BF16), vmem((HD, 128), BF16), vmem((HAL, T), BF16),
         vmem((N_ROW, TB, T), BF16), vmem((HAL + T, T), F32),
         vmem((HD + 16, 128), BF16), vmem((N_CTX, HD + 16, 128), BF16),
         vmem((N_ROW, HD, T), BF16), vmem((N_Y, HD, T), BF16), vmem((N_Y, HD, T), BF16),
-        vmem((N_Y, HD, T), BF16), vmem((N_Y, HD, T), BF16), vmem((N_Y, HD, T), BF16),
-        pltpu.SemaphoreType.REGULAR, pltpu.SemaphoreType.REGULAR((N_CTX,)), dma(11), dma(2), dma(2),
-        *(dma(4) for _ in range(12)),
-        dma(8), dma(8), dma(4), dma(4), dma(8), dma(8), dma(8), dma(8), dma(8), dma(8),
+        vmem((N_Y, HD, T), BF16), vmem((HD, T), BF16), vmem((N_Y, HD, T), BF16), vmem((HD, T), BF16), vmem((N_Y, HD, T), BF16),
+        vmem((N_Y, HD, T), BF16), vmem((N_Y, HD, T), BF16),
+        pltpu.SemaphoreType.REGULAR, pltpu.SemaphoreType.REGULAR((N_CTX,)), dma(14), dma(1), dma(1), dma(8), pltpu.SemaphoreType.DMA,
+        dma(8), dma(8), *(dma(4) for _ in range(8)),
+        dma(8), dma(8), dma(4), dma(4), *(dma(8) for _ in range(12)),
     ]
 
 
 def local(tokens, proj_x, proj_z, proj_bc, proj_dt, dt_bias, decay_rate, skip_gain, conv_x, conv_bc, norm_gain, proj_out):
     hbm = pl.BlockSpec(memory_space=pl.ANY)
-    smem = pl.BlockSpec(memory_space=pltpu.SMEM)
     out = pl.pallas_call(
         kernel,
-        out_shape=jax.ShapeDtypeStruct((HD, T), BF16),
-        in_specs=[hbm] * 9 + [smem] * 3,
-        out_specs=pl.BlockSpec(memory_space=pltpu.VMEM),
+        out_shape=pltpu.VMEM((HD, T), BF16),
+        in_specs=[hbm] * 12,
         scratch_shapes=scratch(),
         compiler_params=pltpu.CompilerParams(collective_id=0, has_side_effects=True),
     )(

time: 40.2 us -> 36.5 us (0.908)
  the two profiles are of different devices: /device:TPU:384 before, /device:TPU:1 now
where the time goes in v3:
time: 36.5 us; the launch traced here: 36.1 us
  Pallas kernels  35.5 us (97%)
  local copies, waits for them, and re-layouts  0.62 us (2%)
    pallas_call x1, Pallas kernels, local(): pl.pallas_call(kernel, out_shape=pltpu.VMEM((HD, T), BF16), in_specs=[hbm...  35.5 us

profile of v3, /device:TPU:1, one launch (start us, length us, event | category | flops | bytes accessed | tf_op | source)
XLA Modules:
  0.0 36.1 jit_solution(15545176763495572177)
XLA Ops:
  0.0 35.5 %shard_map.118 = bf16[64,256]{1,0:T(8,128)(2,1)S(1)} custom-call(bf16[256,1024]{1,0:T(8,128)(2,1)} %tok_h.1, bf16[1024,512]{1,0:T(8,128)(2,1)} %wx_h.1, bf16[1024,512]{1,0:T(8,128)(2,1)} %wz_h.1, bf16[1024,256]{1,0:T(8,128)(2,1)} %wbc_h.1, bf16[8,1024]{1,0:T(8,128)(2,1)} %bitcast.6, bf16[512,1024]{1,0:T(8,128)(2,1)} %wout_h.1, f32[4,512]{1,0:T(4,128)} %bitcast.7, ...), custom_call_target="tpu_custom_call" | custom-call | tf_op jit(solution)/shard_map/pallas_call | solution.py:476
  35.5 0.6 %copy.14 = bf16[256,64]{0,1:T(8,128)(2,1)} copy(bf16[256,64]{0,1:T(8,128)(2,1)S(1)} %bitcast.5) | data formatting | bytes 65536

commit v4 on v3

--- a/solution.py
+++ b/solution.py
@@ -43,31 +43,11 @@
     return v / (1.0 + jnp.exp(-v))
 
 
-class Links:
-    def __init__(self):
-        self.started = []
-
-    def when(self, cond, act):
-        if cond is None:
-            act()
-        else:
-            pl.when(cond)(act)
-
-    def start(self, copy, cond_send=None, cond_recv=None):
-        self.when(cond_send, copy.start)
-        self.started.append([copy, cond_send, cond_recv, True])
-        return len(self.started) - 1
-
-    def arrive(self, k):
-        copy, _, cond, waiting = self.started[k]
-        if waiting and cond is not False:
-            self.when(cond, copy.wait_recv)
-            self.started[k][3] = False
-
-    def finish(self):
-        for k, (copy, cond, _, _) in enumerate(self.started):
-            self.arrive(k)
-            self.when(cond, copy.wait_send)
+def only_when(cond, act):
+    if cond is None:
+        act()
+    else:
+        pl.when(cond)(act)
 
 
 def kernel(
@@ -78,9 +58,9 @@
     bias_s, decay_s, skip_s, eye, tril, prm, prmt, wt,
     pbc, px, pz, rbc, ax, az, sx, sz, rx, rz, xt, xt_in, bt_in, bcraw, bcf,
     st, sr, nb, os, ow, zr, zs, yo, yh, yv, ys, yr,
-    here_y, here_ctx, sem_l, tail_s, tail_r, bt_s, bt_r,
-    bc_s, bc_r, ax_s, ax_r, az_s, az_r, sx_s, sx_r, sz_s, sz_r,
-    gbc_s, gbc_r, st_s, st_r, gn_s, gn_r, z_s, z_r, yo_s, yo_r, yh_s, yh_r, yv_s, yv_r, y_s, y_r,
+    here_y, here_ctx, sem_l,
+    bc_s, ax_s, az_s, sx_s, sz_s, gbc_s, gn_s, z_s, y_s, xt_s, bt_s, st_s,
+    bc_r, sx_r, sz_r, gbc_r, yo_r, y_r, xt_r, bt_r, ax_r, az_r, gn_r, z_r, yh_r, yv_r, st_r,
 ):
     ctx = lax.axis_index("ctx")
     row = lax.axis_index("row")
@@ -151,7 +131,6 @@
             )
         )
     ]
-    links = Links()
     pending = set()
 
     def fetch(*ks):
@@ -167,11 +146,21 @@
                 pending.remove(k)
                 loads[k].wait()
 
-    def done():
-        need(*tuple(pending))
-        present_y()
-        links.finish()
-
+    def begin(copy, cond_send=None, cond_recv=None):
+        only_when(cond_send, copy.start)
+        return copy, cond_recv
+
+    def arrive(begun):
+        copy, cond = begun
+        only_when(cond, copy.wait_recv)
+
+    def all_arrived(ref, rs):
+        remote(ref, ref, rs, rs, row=sibling).wait_recv()
+
+    def all_sent(ref, ss, cond=None):
+        only_when(cond, remote(ref, ref, ss, ss, row=sibling).wait_send)
+
+    sibling = 2 * x + 1 - core
     eye[...] = jnp.where(iota((T, T), 0) == iota((T, T), 1), 1.0, 0.0).astype(BF16)
     tril[...] = jnp.where(iota((T, T), 0) >= iota((T, T), 1), 1.0, 0.0).astype(BF16)
     prm[...] = jnp.zeros(prm.shape, F32)
@@ -180,10 +169,9 @@
     pbc[...] = dot(tok[...], wbc[...]).astype(BF16).reshape(N_ROW, TB, T)
     fetch(5, 6, 7, 8, 9, 11, 12, 13)
     enter()
-    i_bc = {}
     for d in FAR_FIRST_ROW:
         to = rem(row + d, N_ROW)
-        i_bc[d] = links.start(remote(pbc.at[to], rbc.at[d], bc_s.at[d], bc_r.at[d], row=to))
+        begin(remote(pbc.at[to], rbc.at[d], bc_s, bc_r, row=to))
     need(2)
     dt_part = dot_t(wdt[...], tok[...])
     for h in range(N_ROW):
@@ -196,18 +184,18 @@
         return rem(x + d, N_X)
 
     def to_sibling(part, into, ss, rs, d):
-        return links.start(remote(part.at[2 * chip(d) + 1 - core], into.at[d], ss.at[d], rs.at[d], row=2 * x + 1 - core))
+        return begin(remote(part.at[2 * chip(d) + 1 - core], into.at[d], ss, rs.at[d], row=sibling))
 
     def across(part, from_sibling, out, into, ss, rs, d):
         out[d] = (part[2 * chip(d) + core].astype(F32) + from_sibling[d].astype(F32)).astype(BF16)
-        return links.start(remote(out.at[d], into.at[d], ss.at[d], rs.at[d], row=2 * chip(d) + core))
+        return begin(remote(out.at[d], into.at[d], ss, rs, row=2 * chip(d) + core))
 
     def project(w, half, part):
         head = 4 * (b0 + half * (1 - 2 * b0))
         sums = dot(tok[...], w[half]).astype(BF16)
         sums = dot_t(eye[...], sums).astype(BF16)
         for h in range(4):
-            part[head + h, :HD, :] = sums[h * HD : (h + 1) * HD]
+            part[head + h, :HD] = sums[h * HD : (h + 1) * HD]
 
     need(3)
     project(wx, 0, px)
@@ -219,53 +207,33 @@
     need(5)
     project(wz, 0, pz)
     i_az = [to_sibling(pz, az, az_s, az_r, d) for d in order[:2]]
-    i_sx = []
     for k, d in enumerate(order[:2]):
-        links.arrive(i_ax[k])
-        i_sx.append(across(px, ax, sx, rx, sx_s, sx_r, d))
+        arrive(i_ax[k])
+        across(px, ax, sx, rx, sx_s, sx_r, d)
     need(6)
     project(wz, 1, pz)
     i_az += [to_sibling(pz, az, az_s, az_r, d) for d in order[2:]]
-    links.arrive(i_ax[2])
-    i_sx.append(across(px, ax, sx, rx, sx_s, sx_r, order[2]))
+    arrive(i_ax[2])
+    across(px, ax, sx, rx, sx_s, sx_r, order[2])
 
     bc_sum = pbc[row].astype(F32)
-    for d in FAR_FIRST_ROW:
-        links.arrive(i_bc[d])
+    all_arrived(rbc.at[pl.ds(1, N_ROW - 1)], bc_r)
+    for d in range(1, N_ROW):
         bc_sum += rbc[d].astype(F32)
     bcraw[row] = bc_sum.astype(BF16)
-    sibling = 2 * x + 1 - core
-
-    def give(part, peer, source, ss, rs, k):
-        return links.start(remote(part.at[source], part.at[source], ss.at[k], rs.at[k], row=peer))
-
-    def gather_start(part, ss, rs):
-        sent = {d: give(part, 2 * chip(d) + core, row, ss, rs, d) for d in (2, 1, 3)}
-        sent[0] = give(part, sibling, row, ss, rs, 0)
-        return sent
-
-    def gather_pass_on(part, ss, rs, sent):
-        for d in (1, 3, 2):
-            links.arrive(sent[d])
-            sent[4 + d] = give(part, sibling, 2 * chip(N_X - d) + core, ss, rs, 4 + d)
-
-    def gather_end(sent):
-        for k in (0, 5, 7, 6):
-            links.arrive(sent[k])
-
-    i_gbc = [give(bcraw, rem(row + d, N_ROW), row, gbc_s, gbc_r, d) for d in FAR_FIRST_ROW]
-    i_sz = []
+    for d in FAR_FIRST_ROW:
+        begin(remote(bcraw.at[row], bcraw.at[row], gbc_s, gbc_r, row=rem(row + d, N_ROW)))
     for k, d in enumerate(order[:3]):
-        links.arrive(i_az[k])
-        i_sz.append(across(pz, az, sz, rz, sz_s, sz_r, d))
+        arrive(i_az[k])
+        across(pz, az, sz, rz, sz_s, sz_r, d)
     has_next, has_prior, last_row = ctx + 1 < N_CTX, ctx > 0, row == N_ROW - 1
     present_ctx(1, has_next & last_row)
     i_bt = []
     for to in range(N_ROW):
         copy = remote(
-            bcraw.at[row, pl.ds(TB - HAL, HAL)], bt_in, bt_s.at[to], bt_r, ctx=rem(ctx + 1, N_CTX), row=to
+            bcraw.at[row, pl.ds(TB - HAL, HAL)], bt_in, bt_s, bt_r, ctx=rem(ctx + 1, N_CTX), row=to
         )
-        i_bt.append(links.start(copy, has_next & last_row, has_prior if to == 0 else False))
+        i_bt.append(begin(copy, has_next & last_row, has_prior))
 
     need(7, 8, 9, 11, 12, 13)
     lanes = pl.ds(pl.multiple_of((row // 2) * 128, 128), 128)
@@ -282,17 +250,16 @@
             place = jnp.where(zl == side, N_Y + FOR_OWN.index(d), FOR_PARTNER.index(d))
             wt[place] = block[side * HD : (side + 1) * HD]
 
-    links.arrive(i_ax[3])
+    arrive(i_ax[3])
     x_sum = px[row].astype(F32) + ax[0].astype(F32)
-    for k in range(3):
-        links.arrive(i_sx[k])
+    all_arrived(rx.at[pl.ds(1, N_X - 1)], sx_r)
     for d in range(1, N_X):
         x_sum += rx[d].astype(F32)
     x_in = x_sum[:HD]
     xt[...] = x_in[:, 128:].astype(BF16)
     present_ctx(1, has_next & jnp.logical_not(last_row))
-    i_xt = links.start(
-        remote(xt, xt_in, tail_s.at[0], tail_r.at[0], ctx=rem(ctx + 1, N_CTX)), has_next, has_prior
+    i_xt = begin(
+        remote(xt, xt_in, xt_s, xt_r, ctx=rem(ctx + 1, N_CTX)), has_next, has_prior
     )
 
     @pl.when(ctx == 0)
@@ -318,10 +285,9 @@
     keep = iota((T, T), 0) >= iota((T, T), 1)
     weights = jnp.where(keep, jnp.exp(jnp.where(keep, gap, 0.0)), 0.0)
 
-    for k in i_gbc:
-        links.arrive(k)
-
-    links.arrive(i_xt)
+    all_arrived(bcraw.at[pl.ds(1, N_ROW - 1)], gbc_r)
+
+    arrive(i_xt)
     x_cat = jnp.concatenate([xt_in[...].astype(F32), x_in], axis=1)
     acc = col_prm[:, 3:4] * x_in
     for k in range(3):
@@ -330,7 +296,7 @@
     xs = x_conv * dt_row
 
     bcf[HAL:] = bcraw[...].reshape(T, T).astype(F32)
-    links.arrive(i_bt[0])
+    arrive(i_bt[0])
     bcf[:HAL] = bt_in[...].astype(F32)
     acc = cbc[3:4, :] * bcf[HAL : HAL + T]
     for k in range(3):
@@ -347,8 +313,8 @@
     for d in (2, 3, 1):
         if d > 1:
             present_ctx(d, ctx + d < N_CTX)
-        copy = remote(st, sr.at[d], st_s.at[d], st_r.at[d], ctx=rem(ctx + d, N_CTX))
-        i_st[d] = links.start(copy, ctx + d < N_CTX, ctx >= d)
+        copy = remote(st, sr.at[d], st_s.at[d - 1], st_r.at[d - 1], ctx=rem(ctx + d, N_CTX))
+        i_st[d] = begin(copy, ctx + d < N_CTX, ctx >= d)
 
         @pl.when(ctx < d)
         def _():
@@ -357,15 +323,14 @@
     scores = dot_t(c_mat, b_mat)
     inner = dot_t(xs.astype(BF16), (scores * weights).astype(BF16))
     partial_out = inner + skip_s[row] * x_conv
-    links.arrive(i_az[3])
+    arrive(i_az[3])
     z_in = pz[row].astype(F32) + az[0].astype(F32)
-    for k in range(3):
-        links.arrive(i_sz[k])
+    all_arrived(rz.at[pl.ds(1, N_X - 1)], sz_r)
     for d in range(1, N_X):
         z_in += rz[d].astype(F32)
     gate = silu(z_in)
     for d in (1, 3, 2):
-        links.arrive(i_st[d])
+        arrive(i_st[d])
 
     def log_of(d):
         return (sr[d, HD : HD + 8].astype(F32) + sr[d, HD + 8 :].astype(F32))[0:1]
@@ -378,9 +343,15 @@
     inv = lax.rsqrt(jnp.sum(gated * gated, axis=0, keepdims=True) * (1.0 / HD) + 1e-05)
     nb[row] = (gated * inv * col_prm[:, 4:5]).astype(BF16)
 
-    i_gn = gather_start(nb, gn_s, gn_r)
-    gather_pass_on(nb, gn_s, gn_r, i_gn)
-    gather_end(i_gn)
+    def give(peer, source, rs):
+        return begin(remote(nb.at[source], nb.at[source], gn_s, rs, row=peer))
+
+    i_gn = {d: give(2 * chip(d) + core, row, gn_r.at[d]) for d in (2, 1, 3)}
+    give(sibling, row, gn_r.at[0])
+    for d in (1, 3, 2):
+        arrive(i_gn[d])
+        give(sibling, 2 * chip(N_X - d) + core, gn_r.at[0])
+    all_arrived(nb.at[pl.ds(0, N_X)], gn_r.at[0])
 
     heads = nb[...].reshape(N_ROW * HD, T)
 
@@ -388,62 +359,83 @@
         part = dot(wt[first : first + 4].reshape(4 * HD, N_ROW * HD), heads)
         into[at : at + 4] = part.astype(BF16).reshape(4, HD, T)
 
-    def to_partner(src, k):
-        return links.start(remote(src, zr.at[k], z_s.at[k], z_r.at[k], col=col + 1 - 2 * zl))
-
-    def along_y_to(src, into, ss, rs, d):
-        return links.start(remote(src, into, ss, rs, col=(rem(y + d, N_Y)) * 2 + zl))
-
-    def along_y(src, into, ss, rs, d):
-        return along_y_to(src, into.at[d], ss.at[d], rs.at[d], d)
+    def along_y(src, into, rs, d):
+        return begin(remote(src, into, y_s, rs, col=rem(y + d, N_Y) * 2 + zl))
+
+    halves = (slice(0, HD // 2), slice(HD // 2, HD))
+    i_z = {}
+
+    def send_z(d, side):
+        k = FOR_PARTNER.index(d)
+        rows = halves[side]
+        i_z[d, side] = begin(
+            remote(os.at[k, rows], zr.at[k, rows], z_s, z_r.at[2 * k + side], col=col + 1 - 2 * zl)
+        )
 
     blocks(0, os, 0)
-    i_z = [to_partner(os.at[k], k) for k in range(4)]
+    for d, side in ((4, 0), (4, 1), (3, 0), (5, 0), (3, 1), (5, 1), (2, 0), (2, 1)):
+        send_z(d, side)
     blocks(4, os, 4)
-    i_z.append(to_partner(os.at[4], 4))
+    send_z(6, 0)
+    send_z(6, 1)
     present_y()
-    i_yo = [along_y(os.at[FOR_PARTNER.index(d)], yo, yo_s, yo_r, d) for d in (1, 7)]
+    for k, d in enumerate((1, 7)):
+        along_y(os.at[FOR_PARTNER.index(d)], yo.at[k], yo_r, d)
     blocks(N_Y, ow, 0)
-    i_y = [along_y(ow.at[FOR_OWN.index(d)], yr, y_s, y_r, d) for d in (1, 7)]
+    for k, d in enumerate((1, 7)):
+        along_y(ow.at[FOR_OWN.index(d)], yr.at[k], y_r, d)
     blocks(N_Y + 4, ow, 4)
-    i_near = {}
-    for k, d in enumerate(FOR_PARTNER[:5]):
-        if k == 2:
-            links.arrive(i_yo[0])
-            links.arrive(i_yo[1])
-            zs[...] = (os[7].astype(F32) + yo[1].astype(F32) + yo[7].astype(F32)).astype(BF16)
-            i_z0 = to_partner(zs, 7)
-        links.arrive(i_z[k])
-        own = ow[FOR_OWN.index(d)].astype(F32) + zr[k].astype(F32)
-        if d not in (2, 6):
-            ys[d] = own.astype(BF16)
-        if d in (3, 5):
-            to, on = (1, 2) if d == 3 else (7, 6)
-            i_near[on] = along_y_to(ys.at[d], yv.at[on], yv_s.at[on], yv_r.at[on], to)
-            continue
-        if d == 4:
-            i_half = {}
-            for to, at in ((2, 0), (6, HD // 2)):
-                rows = pl.ds(at, HD // 2)
-                i_half[to] = along_y_to(ys.at[4, rows], yh.at[rows], yh_s.at[to], yh_r.at[to], to)
-            continue
-        if d in (2, 6):
-            links.arrive(i_half[d])
-            links.arrive(i_near[d])
-            lo = slice(0, HD // 2), slice(HD // 2, HD)
-            for side, rows in ((2, lo[0]), (6, lo[1])):
-                more = own[rows] + yv[d, rows].astype(F32)
-                ys[d, rows] = (more + yh[rows].astype(F32) if side == d else more).astype(BF16)
-        i_y.append(along_y(ys.at[d], yr, y_s, y_r, d))
-    links.arrive(i_z0)
+
+    def pair_sum(d, side):
+        arrive(i_z[d, side])
+        rows = halves[side]
+        return ow[FOR_OWN.index(d), rows].astype(F32) + zr[FOR_PARTNER.index(d), rows].astype(F32)
+
+    i_half, i_near = {}, {}
+    for side, to in ((0, 2), (1, 6)):
+        rows = halves[side]
+        ys[4, rows] = pair_sum(4, side).astype(BF16)
+        i_half[to, side] = along_y(ys.at[4, rows], yh.at[rows], yh_r.at[side], to)
+    for side in range(2):
+        for d, to, on in ((3, 1, 2), (5, 7, 6)):
+            rows, at = halves[side], (on - 2) // 4
+            ys[d, rows] = pair_sum(d, side).astype(BF16)
+            i_near[on, side] = along_y(ys.at[d, rows], yv.at[at, rows], yv_r.at[2 * at + side], to)
+    all_arrived(yo, yo_r)
+    zs[...] = (os[7].astype(F32) + yo[0].astype(F32) + yo[1].astype(F32)).astype(BF16)
+    i_z0 = begin(remote(zs, zr.at[7], z_s, z_r.at[10], col=col + 1 - 2 * zl))
+    for side in range(2):
+        for d in (2, 6):
+            rows, at = halves[side], (d - 2) // 4
+            more = pair_sum(d, side)
+            arrive(i_near[d, side])
+            more += yv[at, rows].astype(F32)
+            if (d, side) in i_half:
+                arrive(i_half[d, side])
+                more += yh[rows].astype(F32)
+            ys[d, rows] = more.astype(BF16)
+            along_y(ys.at[d, rows], yr.at[2 + at, rows], y_r, d)
+    arrive(i_z0)
     result = ow[7].astype(F32) + zr[7].astype(F32)
-    for k in i_y:
-        links.arrive(k)
-    for d in (1, 2, 6, 7):
-        result += yr[d].astype(F32)
+    all_arrived(yr, y_r)
+    for k in range(4):
+        result += yr[k].astype(F32)
     out_ref[...] = result.astype(BF16)
 
-    done()
+    need(*tuple(pending))
+    all_sent(pbc.at[pl.ds(0, 7)], bc_s)
+    all_sent(px.at[pl.ds(0, 4)], ax_s)
+    all_sent(pz.at[pl.ds(0, 4)], az_s)
+    all_sent(sx.at[pl.ds(0, 3)], sx_s)
+    all_sent(sz.at[pl.ds(0, 3)], sz_s)
+    all_sent(bcraw.at[pl.ds(0, 7)], gbc_s)
+    all_sent(nb.at[pl.ds(0, 7)], gn_s)
+    all_sent(os.at[pl.ds(0, 6)], z_s)
+    all_sent(wt.at[pl.ds(0, 9), :, pl.ds(0, T)], y_s)
+    all_sent(xt, xt_s, has_next)
+    all_sent(bcraw.at[pl.ds(0, 4)], bt_s, has_next & last_row)
+    for d in range(1, N_CTX):
+        all_sent(st, st_s.at[d - 1], ctx + d < N_CTX)
 
 
 def scratch():
@@ -463,11 +455,11 @@
         vmem((N_ROW, TB, T), BF16), vmem((HAL + T, T), F32),
         vmem((HD + 16, 128), BF16), vmem((N_CTX, HD + 16, 128), BF16),
         vmem((N_ROW, HD, T), BF16), vmem((N_Y, HD, T), BF16), vmem((N_Y, HD, T), BF16),
-        vmem((N_Y, HD, T), BF16), vmem((HD, T), BF16), vmem((N_Y, HD, T), BF16), vmem((HD, T), BF16), vmem((N_Y, HD, T), BF16),
-        vmem((N_Y, HD, T), BF16), vmem((N_Y, HD, T), BF16),
-        pltpu.SemaphoreType.REGULAR, pltpu.SemaphoreType.REGULAR((N_CTX,)), dma(14), dma(1), dma(1), dma(8), pltpu.SemaphoreType.DMA,
-        dma(8), dma(8), *(dma(4) for _ in range(8)),
-        dma(8), dma(8), dma(4), dma(4), *(dma(8) for _ in range(12)),
+        vmem((N_Y, HD, T), BF16), vmem((HD, T), BF16), vmem((2, HD, T), BF16), vmem((HD, T), BF16), vmem((2, HD, T), BF16),
+        vmem((N_Y, HD, T), BF16), vmem((4, HD, T), BF16),
+        pltpu.SemaphoreType.REGULAR, pltpu.SemaphoreType.REGULAR((N_CTX,)), dma(14),
+        *(pltpu.SemaphoreType.DMA for _ in range(11)), dma(3),
+        *(pltpu.SemaphoreType.DMA for _ in range(8)), dma(4), dma(4), dma(4), dma(11), dma(2), dma(4), dma(3),
     ]
 
 

time: 36.5 us -> 34.9 us (0.956)
  the two profiles are of different devices: /device:TPU:1 before, /device:TPU:401 now
where the time goes in v4:
time: 34.9 us; the launch traced here: 34.8 us
  Pallas kernels  34.2 us (98%)
  local copies, waits for them, and re-layouts  0.62 us (2%)
    pallas_call x1, Pallas kernels, local(): pl.pallas_call(kernel, out_shape=pltpu.VMEM((HD, T), BF16), in_specs=[hbm...  34.2 us

profile of v4, /device:TPU:401, one launch (start us, length us, event | category | flops | bytes accessed | tf_op | source)
XLA Modules:
  0.0 34.8 jit_solution(3823958121929606668)
XLA Ops:
  0.0 34.2 %shard_map.118 = bf16[64,256]{1,0:T(8,128)(2,1)S(1)} custom-call(bf16[256,1024]{1,0:T(8,128)(2,1)} %tok_h.1, bf16[1024,512]{1,0:T(8,128)(2,1)} %wx_h.1, bf16[1024,512]{1,0:T(8,128)(2,1)} %wz_h.1, bf16[1024,256]{1,0:T(8,128)(2,1)} %wbc_h.1, bf16[8,1024]{1,0:T(8,128)(2,1)} %bitcast.6, bf16[512,1024]{1,0:T(8,128)(2,1)} %wout_h.1, f32[4,512]{1,0:T(4,128)} %bitcast.7, ...), custom_call_target="tpu_custom_call" | custom-call | tf_op jit(solution)/shard_map/pallas_call | solution.py:468
  34.2 0.6 %copy.14 = bf16[256,64]{0,1:T(8,128)(2,1)} copy(bf16[256,64]{0,1:T(8,128)(2,1)S(1)} %bitcast.5) | data formatting | bytes 65536

commit v5 on v4

--- a/solution.py
+++ b/solution.py
@@ -60,7 +60,7 @@
     st, sr, nb, os, ow, zr, zs, yo, yh, yv, ys, yr,
     here_y, here_ctx, sem_l,
     bc_s, ax_s, az_s, sx_s, sz_s, gbc_s, gn_s, z_s, y_s, xt_s, bt_s, st_s,
-    bc_r, sx_r, sz_r, gbc_r, yo_r, y_r, xt_r, bt_r, ax_r, az_r, gn_r, z_r, yh_r, yv_r, st_r,
+    bc_r, sx_r, sz_r, gbc_r, yo_r, y_r, xt_r, bt_r, az_r, ax_r, gn_r, z_r, yh_r, yv_r, st_r,
 ):
     ctx = lax.axis_index("ctx")
     row = lax.axis_index("row")
@@ -184,7 +184,7 @@
         return rem(x + d, N_X)
 
     def to_sibling(part, into, ss, rs, d):
-        return begin(remote(part.at[2 * chip(d) + 1 - core], into.at[d], ss, rs.at[d], row=sibling))
+        begin(remote(part.at[2 * chip(d) + 1 - core], into.at[d], ss, rs, row=sibling))
 
     def across(part, from_sibling, out, into, ss, rs, d):
         out[d] = (part[2 * chip(d) + core].astype(F32) + from_sibling[d].astype(F32)).astype(BF16)
@@ -199,21 +199,25 @@
 
     need(3)
     project(wx, 0, px)
-    i_ax = [to_sibling(px, ax, ax_s, ax_r, d) for d in order[:2]]
+    for d in order[:2]:
+        to_sibling(px, ax, ax_s, ax_r.at[0], d)
     need(4)
     project(wx, 1, px)
-    i_ax += [to_sibling(px, ax, ax_s, ax_r, d) for d in order[2:]]
+    for d in order[2:]:
+        to_sibling(px, ax, ax_s, ax_r.at[1], d)
     fetch(10)
     need(5)
     project(wz, 0, pz)
-    i_az = [to_sibling(pz, az, az_s, az_r, d) for d in order[:2]]
-    for k, d in enumerate(order[:2]):
-        arrive(i_ax[k])
+    for d in order[:2]:
+        to_sibling(pz, az, az_s, az_r, d)
+    all_arrived(ax.at[pl.ds(0, 2)], ax_r.at[0])
+    for d in order[:2]:
         across(px, ax, sx, rx, sx_s, sx_r, d)
     need(6)
     project(wz, 1, pz)
-    i_az += [to_sibling(pz, az, az_s, az_r, d) for d in order[2:]]
-    arrive(i_ax[2])
+    for d in order[2:]:
+        to_sibling(pz, az, az_s, az_r, d)
+    all_arrived(ax.at[pl.ds(0, 2)], ax_r.at[1])
     across(px, ax, sx, rx, sx_s, sx_r, order[2])
 
     bc_sum = pbc[row].astype(F32)
@@ -223,8 +227,8 @@
     bcraw[row] = bc_sum.astype(BF16)
     for d in FAR_FIRST_ROW:
         begin(remote(bcraw.at[row], bcraw.at[row], gbc_s, gbc_r, row=rem(row + d, N_ROW)))
-    for k, d in enumerate(order[:3]):
-        arrive(i_az[k])
+    all_arrived(az, az_r)
+    for d in order[:3]:
         across(pz, az, sz, rz, sz_s, sz_r, d)
     has_next, has_prior, last_row = ctx + 1 < N_CTX, ctx > 0, row == N_ROW - 1
     present_ctx(1, has_next & last_row)
@@ -235,22 +239,7 @@
         )
         i_bt.append(begin(copy, has_next & last_row, has_prior))
 
-    need(7, 8, 9, 11, 12, 13)
-    lanes = pl.ds(pl.multiple_of((row // 2) * 128, 128), 128)
-    prm[0:4, :] = cx[:, lanes]
-    prm[4:5, :] = gain[:, lanes]
-    prmt[...] = prm[...].T
-    col_prm = prmt[pl.ds(pl.multiple_of((row % 2) * HD, HD), HD), :]
-
-    need(10)
-    for d in range(N_Y):
-        lanes = pl.ds(pl.multiple_of((rem(y + d, N_Y)) * 128, 128), 128)
-        block = dot_t(eye[:128, :128], wout[:, lanes]).astype(BF16)
-        for side in range(2):
-            place = jnp.where(zl == side, N_Y + FOR_OWN.index(d), FOR_PARTNER.index(d))
-            wt[place] = block[side * HD : (side + 1) * HD]
-
-    arrive(i_ax[3])
+    need(11, 12, 13)
     x_sum = px[row].astype(F32) + ax[0].astype(F32)
     all_arrived(rx.at[pl.ds(1, N_X - 1)], sx_r)
     for d in range(1, N_X):
@@ -285,6 +274,21 @@
     keep = iota((T, T), 0) >= iota((T, T), 1)
     weights = jnp.where(keep, jnp.exp(jnp.where(keep, gap, 0.0)), 0.0)
 
+    need(7, 8, 9)
+    lanes = pl.ds(pl.multiple_of((row // 2) * 128, 128), 128)
+    prm[0:4, :] = cx[:, lanes]
+    prm[4:5, :] = gain[:, lanes]
+    prmt[...] = prm[...].T
+    col_prm = prmt[pl.ds(pl.multiple_of((row % 2) * HD, HD), HD), :]
+
+    need(10)
+    for d in range(N_Y):
+        lanes = pl.ds(pl.multiple_of((rem(y + d, N_Y)) * 128, 128), 128)
+        block = dot_t(eye[:128, :128], wout[:, lanes]).astype(BF16)
+        for side in range(2):
+            place = jnp.where(zl == side, N_Y + FOR_OWN.index(d), FOR_PARTNER.index(d))
+            wt[place] = block[side * HD : (side + 1) * HD]
+
     all_arrived(bcraw.at[pl.ds(1, N_ROW - 1)], gbc_r)
 
     arrive(i_xt)
@@ -323,7 +327,6 @@
     scores = dot_t(c_mat, b_mat)
     inner = dot_t(xs.astype(BF16), (scores * weights).astype(BF16))
     partial_out = inner + skip_s[row] * x_conv
-    arrive(i_az[3])
     z_in = pz[row].astype(F32) + az[0].astype(F32)
     all_arrived(rz.at[pl.ds(1, N_X - 1)], sz_r)
     for d in range(1, N_X):
@@ -348,6 +351,17 @@
 
     i_gn = {d: give(2 * chip(d) + core, row, gn_r.at[d]) for d in (2, 1, 3)}
     give(sibling, row, gn_r.at[0])
+
+    all_sent(pbc.at[pl.ds(0, 7)], bc_s)
+    all_sent(px.at[pl.ds(0, 4)], ax_s)
+    all_sent(pz.at[pl.ds(0, 4)], az_s)
+    all_sent(sx.at[pl.ds(0, 3)], sx_s)
+    all_sent(sz.at[pl.ds(0, 3)], sz_s)
+    all_sent(bcraw.at[pl.ds(0, 7)], gbc_s)
+    all_sent(xt, xt_s, has_next)
+    all_sent(bcraw.at[pl.ds(0, 4)], bt_s, has_next & last_row)
+    for d in range(1, N_CTX):
+        all_sent(st, st_s.at[d - 1], ctx + d < N_CTX)
     for d in (1, 3, 2):
         arrive(i_gn[d])
         give(sibling, 2 * chip(N_X - d) + core, gn_r.at[0])
@@ -363,14 +377,11 @@
         return begin(remote(src, into, y_s, rs, col=rem(y + d, N_Y) * 2 + zl))
 
     halves = (slice(0, HD // 2), slice(HD // 2, HD))
-    i_z = {}
 
     def send_z(d, side):
-        k = FOR_PARTNER.index(d)
-        rows = halves[side]
-        i_z[d, side] = begin(
-            remote(os.at[k, rows], zr.at[k, rows], z_s, z_r.at[2 * k + side], col=col + 1 - 2 * zl)
-        )
+        k, rows = FOR_PARTNER.index(d), halves[side]
+        rs = z_r.at[side if d == 4 else 4 if d in (2, 6) else 2 + side]
+        begin(remote(os.at[k, rows], zr.at[k, rows], z_s, rs, col=col + 1 - 2 * zl))
 
     blocks(0, os, 0)
     for d, side in ((4, 0), (4, 1), (3, 0), (5, 0), (3, 1), (5, 1), (2, 0), (2, 1)):
@@ -385,25 +396,28 @@
     for k, d in enumerate((1, 7)):
         along_y(ow.at[FOR_OWN.index(d)], yr.at[k], y_r, d)
     blocks(N_Y + 4, ow, 4)
+    all_sent(nb.at[pl.ds(0, 7)], gn_s)
 
     def pair_sum(d, side):
-        arrive(i_z[d, side])
         rows = halves[side]
         return ow[FOR_OWN.index(d), rows].astype(F32) + zr[FOR_PARTNER.index(d), rows].astype(F32)
 
     i_half, i_near = {}, {}
     for side, to in ((0, 2), (1, 6)):
         rows = halves[side]
+        all_arrived(zr.at[0, rows], z_r.at[side])
         ys[4, rows] = pair_sum(4, side).astype(BF16)
         i_half[to, side] = along_y(ys.at[4, rows], yh.at[rows], yh_r.at[side], to)
     for side in range(2):
+        all_arrived(zr.at[0], z_r.at[2 + side])
         for d, to, on in ((3, 1, 2), (5, 7, 6)):
             rows, at = halves[side], (on - 2) // 4
             ys[d, rows] = pair_sum(d, side).astype(BF16)
             i_near[on, side] = along_y(ys.at[d, rows], yv.at[at, rows], yv_r.at[2 * at + side], to)
     all_arrived(yo, yo_r)
     zs[...] = (os[7].astype(F32) + yo[0].astype(F32) + yo[1].astype(F32)).astype(BF16)
-    i_z0 = begin(remote(zs, zr.at[7], z_s, z_r.at[10], col=col + 1 - 2 * zl))
+    i_z0 = begin(remote(zs, zr.at[7], z_s, z_r.at[5], col=col + 1 - 2 * zl))
+    all_arrived(zr.at[pl.ds(0, 2)], z_r.at[4])
     for side in range(2):
         for d in (2, 6):
             rows, at = halves[side], (d - 2) // 4
@@ -423,19 +437,8 @@
     out_ref[...] = result.astype(BF16)
 
     need(*tuple(pending))
-    all_sent(pbc.at[pl.ds(0, 7)], bc_s)
-    all_sent(px.at[pl.ds(0, 4)], ax_s)
-    all_sent(pz.at[pl.ds(0, 4)], az_s)
-    all_sent(sx.at[pl.ds(0, 3)], sx_s)
-    all_sent(sz.at[pl.ds(0, 3)], sz_s)
-    all_sent(bcraw.at[pl.ds(0, 7)], gbc_s)
-    all_sent(nb.at[pl.ds(0, 7)], gn_s)
     all_sent(os.at[pl.ds(0, 6)], z_s)
     all_sent(wt.at[pl.ds(0, 9), :, pl.ds(0, T)], y_s)
-    all_sent(xt, xt_s, has_next)
-    all_sent(bcraw.at[pl.ds(0, 4)], bt_s, has_next & last_row)
-    for d in range(1, N_CTX):
-        all_sent(st, st_s.at[d - 1], ctx + d < N_CTX)
 
 
 def scratch():
@@ -459,7 +462,7 @@
         vmem((N_Y, HD, T), BF16), vmem((4, HD, T), BF16),
         pltpu.SemaphoreType.REGULAR, pltpu.SemaphoreType.REGULAR((N_CTX,)), dma(14),
         *(pltpu.SemaphoreType.DMA for _ in range(11)), dma(3),
-        *(pltpu.SemaphoreType.DMA for _ in range(8)), dma(4), dma(4), dma(4), dma(11), dma(2), dma(4), dma(3),
+        *(pltpu.SemaphoreType.DMA for _ in range(9)), dma(2), dma(4), dma(6), dma(2), dma(4), dma(3),
     ]
 
 

time: 34.9 us -> 34.9 us (level)
  the two profiles are of different devices: /device:TPU:401 before, /device:TPU:1 now
where the time goes in v5:
time: 34.9 us; the launch traced here: 34.5 us
  Pallas kernels  33.8 us (97%)
  local copies, waits for them, and re-layouts  0.62 us (2%)
    pallas_call x1, Pallas kernels, local(): pl.pallas_call(kernel, out_shape=pltpu.VMEM((HD, T), BF16), in_specs=[hbm...  33.8 us

profile of v5, /device:TPU:1, one launch (start us, length us, event | category | flops | bytes accessed | tf_op | source)
XLA Modules:
  0.0 34.5 jit_solution(10911028447970652872)
XLA Ops:
  0.0 33.8 %shard_map.118 = bf16[64,256]{1,0:T(8,128)(2,1)S(1)} custom-call(bf16[256,1024]{1,0:T(8,128)(2,1)} %tok_h.1, bf16[1024,512]{1,0:T(8,128)(2,1)} %wx_h.1, bf16[1024,512]{1,0:T(8,128)(2,1)} %wz_h.1, bf16[1024,256]{1,0:T(8,128)(2,1)} %wbc_h.1, bf16[8,1024]{1,0:T(8,128)(2,1)} %bitcast.6, bf16[512,1024]{1,0:T(8,128)(2,1)} %wout_h.1, f32[4,512]{1,0:T(4,128)} %bitcast.7, ...), custom_call_target="tpu_custom_call" | custom-call | tf_op jit(solution)/shard_map/pallas_call | solution.py:471
  33.9 0.6 %copy.14 = bf16[256,64]{0,1:T(8,128)(2,1)} copy(bf16[256,64]{0,1:T(8,128)(2,1)S(1)} %bitcast.5) | data formatting | bytes 65536

commit v6 on v5

--- a/solution.py
+++ b/solution.py
@@ -379,16 +379,15 @@
     halves = (slice(0, HD // 2), slice(HD // 2, HD))
 
     def send_z(d, side):
-        k, rows = FOR_PARTNER.index(d), halves[side]
+        k, rows = FOR_PARTNER.index(d), slice(0, HD) if d in (2, 6) else halves[side]
         rs = z_r.at[side if d == 4 else 4 if d in (2, 6) else 2 + side]
         begin(remote(os.at[k, rows], zr.at[k, rows], z_s, rs, col=col + 1 - 2 * zl))
 
     blocks(0, os, 0)
-    for d, side in ((4, 0), (4, 1), (3, 0), (5, 0), (3, 1), (5, 1), (2, 0), (2, 1)):
+    for d, side in ((4, 0), (4, 1), (3, 0), (5, 0), (3, 1), (5, 1), (2, 0)):
         send_z(d, side)
     blocks(4, os, 4)
     send_z(6, 0)
-    send_z(6, 1)
     present_y()
     for k, d in enumerate((1, 7)):
         along_y(os.at[FOR_PARTNER.index(d)], yo.at[k], yo_r, d)

time: 34.9 us -> 34.9 us (level)
  no operation moved by 1% of the time
where the time goes in v6:
time: 34.9 us; the launch traced here: 34.5 us
  Pallas kernels  33.8 us (97%)
  local copies, waits for them, and re-layouts  0.62 us (2%)
    pallas_call x1, Pallas kernels, local(): pl.pallas_call(kernel, out_shape=pltpu.VMEM((HD, T), BF16), in_specs=[hbm...  33.8 us

profile of v6, /device:TPU:1, one launch (start us, length us, event | category | flops | bytes accessed | tf_op | source)
XLA Modules:
  0.0 34.5 jit_solution(11069865518814632607)
XLA Ops:
  0.0 33.8 %shard_map.118 = bf16[64,256]{1,0:T(8,128)(2,1)S(1)} custom-call(bf16[256,1024]{1,0:T(8,128)(2,1)} %tok_h.1, bf16[1024,512]{1,0:T(8,128)(2,1)} %wx_h.1, bf16[1024,512]{1,0:T(8,128)(2,1)} %wz_h.1, bf16[1024,256]{1,0:T(8,128)(2,1)} %wbc_h.1, bf16[8,1024]{1,0:T(8,128)(2,1)} %bitcast.6, bf16[512,1024]{1,0:T(8,128)(2,1)} %wout_h.1, f32[4,512]{1,0:T(4,128)} %bitcast.7, ...), custom_call_target="tpu_custom_call" | custom-call | tf_op jit(solution)/shard_map/pallas_call | solution.py:470
  33.9 0.6 %copy.14 = bf16[256,64]{0,1:T(8,128)(2,1)} copy(bf16[256,64]{0,1:T(8,128)(2,1)S(1)} %bitcast.5) | data formatting | bytes 65536
